TPU v7x, 512 devices: a whole 4x4x16 slice. The times are simulated.
512 devices in a mesh: gx: 128 (over y_hi, x, z), gy: 4 (over y_lo, core).
Axes of the slice: x: 4, y: 4 (y_hi: 2, y_lo: 2; y = y_hi * 2 + y_lo), z: 16, core: 2. Of those that a mesh axis runs over, the one named last changes fastest.
Arguments:
- trans: float32 [13, 256, 4096], P(None, 'gx', 'gy'), may hold values from 0.1 to 1
- storage: float32 [256, 4096], P('gx', 'gy'), may hold values from 0.05 to 1
- fault_cells: int32 [128, 4, 512], P('gx', 'gy'), may hold values from 0 to 2047, as said below
- fault_count: int32 [128, 4], P('gx', 'gy'), may hold values from 0 to 512, as said below
- fault_trans: float32 [128, 4, 512], P('gx', 'gy'), may hold values from 0.1 to 1, as said below
Outputs:
- coarse_columns: float32 [125, 128, 1024], P(None, 'gx', 'gy')
Inputs may be any that keep to these rules, and one draw needn't show every extreme that they name: `fault_cells`: on a device with even gx index every slot's cell lies at x' = 1, on one with odd gx index at x' = 0; slot k of the partners with gx indices 2j and 2j + 1 (same gy index) has equal y' and layers z differing by at most 8. `fault_count`: equal on devices whose gx indices are 2j and 2j + 1 with the same gy index; some device has 512. `fault_trans`: equal slot by slot on devices whose gx indices are 2j and 2j + 1 with the same gy index.
All inputs are finite; a program needn't handle non-finite values.
Results may differ from a plain program's by a relative error of at most 0.0003.
Values sent between devices are 32-bit elements; how exact they have to be, the bound alone decides.
A program may use at most 64 MiB of HBM per device.

v0:
```python
import jax
import jax.numpy as jnp
from jax import lax
from jax.sharding import PartitionSpec as P

NZ = 128
COLORS = 125


FORWARD = (
    (0, 0, 1),
    (0, 1, -1),
    (0, 1, 0),
    (0, 1, 1),
    (1, -1, -1),
    (1, -1, 0),
    (1, -1, 1),
    (1, 0, -1),
    (1, 0, 0),
    (1, 0, 1),
    (1, 1, -1),
    (1, 1, 0),
    (1, 1, 1),
)
damping = 2.0 / 3.0
tentative_value = 0.35355339059327373


def with_halo(value, sides, width):
    for axis, dim in sides:
        peers, length = (lax.axis_size(axis), value.shape[dim])
        up = [(i, (i + 1) % peers) for i in range(peers - 1)]
        down = [(j, i) for i, j in up]
        last = lax.slice_in_dim(value, length - width, length, axis=dim)
        leading = lax.slice_in_dim(value, 0, width, axis=dim)
        before = lax.ppermute(last, axis, up)
        after = lax.ppermute(leading, axis, down)
        value = jnp.concatenate([before, value, after], axis=dim)
    return value


def from_partner(value, axis, stride):
    mask = 2**stride
    pairs = [(source, source ^ mask) for source in range(lax.axis_size(axis))]
    return lax.ppermute(value, axis, pairs)


def build_probes(coord_x, coord_y, coord_z, grid_x, grid_y):
    colour = jnp.arange(COLORS, dtype=jnp.int32)[:, None, None, None]
    agrees = (
        (coord_x // 2 % 5 == colour // 25)
        & (coord_y // 2 % 5 == colour // 5 % 5)
        & (coord_z // 2 % 5 == colour % 5)
    )
    inside = (coord_x >= 0) & (coord_x < grid_x) & (coord_y >= 0) & (coord_y < grid_y)
    return jnp.where(agrees & inside, jnp.float32(tentative_value), jnp.float32(0.0))


def depth_pad(field):
    return jnp.pad(field, ((0, 0), (0, 0), (0, 0), (1, 1)))


def per_device(trans, storage, fault_cells, fault_count, fault_trans):
    layers = NZ
    cells_x = trans.shape[1]
    cells_y = trans.shape[2] // layers
    cell_count = cells_x * cells_y * layers
    grid_x = cells_x * lax.axis_size("gx")
    grid_y = cells_y * lax.axis_size("gy")
    start_x = lax.axis_index("gx") * cells_x
    start_y = lax.axis_index("gy") * cells_y
    coord_x = start_x + jnp.arange(cells_x, dtype=jnp.int32)[:, None, None]
    coord_y = start_y + jnp.arange(cells_y, dtype=jnp.int32)[None, :, None]
    coord_z = jnp.arange(layers, dtype=jnp.int32)[None, None, :]
    weights = trans.reshape(13, cells_x, cells_y, layers)
    pieces = []
    for offset, step in enumerate(FORWARD):
        inside = (
            (coord_x + step[0] >= 0)
            & (coord_x + step[0] < grid_x)
            & (coord_y + step[1] >= 0)
            & (coord_y + step[1] < grid_y)
            & (coord_z + step[2] >= 0)
            & (coord_z + step[2] < layers)
        )
        pieces.append(jnp.where(inside, weights[offset], jnp.float32(0.0)))
    masked = jnp.stack(pieces)
    rim_depth = 1
    widened = with_halo(masked, (("gx", 1), ("gy", 2)), rim_depth)
    widened = depth_pad(widened)

    def window(array, margin, step_x, step_y, step_z, edge):
        low_x = margin - edge + step_x
        low_y = margin - edge + step_y
        return array[
            ...,
            low_x : low_x + cells_x + 2 * edge,
            low_y : low_y + cells_y + 2 * edge,
            1 + step_z : 1 + step_z + layers,
        ]

    behind_sum = jnp.zeros((cells_x, cells_y, layers), jnp.float32)
    for offset, step in enumerate(FORWARD):
        behind_sum = behind_sum + window(
            widened[offset], rim_depth, -step[0], -step[1], -step[2], 0
        )
    fault_flat = fault_cells.reshape(-1)
    slots = jnp.arange(fault_flat.shape[0], dtype=jnp.int32)
    live_trans = jnp.where(
        slots < fault_count.reshape(()), fault_trans.reshape(-1), jnp.float32(0.0)
    )
    one_hot = (fault_flat[:, None] == jnp.arange(cell_count, dtype=jnp.int32)[None, :]).astype(
        jnp.float32
    )
    fault_diag = jnp.dot(live_trans, one_hot, precision=lax.Precision.HIGHEST).reshape(
        cells_x, cells_y, layers
    )
    diagonal = (
        storage.reshape(cells_x, cells_y, layers) + jnp.sum(masked, 0) + behind_sum + fault_diag
    )

    def stencil(padded, margin, edge, diag_region):
        summed = diag_region * window(padded, margin, 0, 0, 0, edge)
        for offset, step in enumerate(FORWARD):
            summed = (
                summed
                - window(widened[offset], rim_depth, 0, 0, 0, edge)
                * window(padded, margin, step[0], step[1], step[2], edge)
                - window(widened[offset], rim_depth, -step[0], -step[1], -step[2], edge)
                * window(padded, margin, -step[0], -step[1], -step[2], edge)
            )
        return summed

    def fault_term(center):
        own_values = jnp.take(center.reshape(center.shape[0], cell_count), fault_flat, axis=1)
        partner_values = from_partner(own_values, "gx", 0)
        across = jnp.dot(
            partner_values * live_trans[None, :], one_hot, precision=lax.Precision.HIGHEST
        )
        return across.reshape(center.shape)

    def extend(field):
        return with_halo(field, (("gx", 1), ("gy", 2)), 1)

    probes = build_probes(coord_x, coord_y, coord_z, grid_x, grid_y)
    outer_x = start_x - 1 + jnp.arange(cells_x + 2, dtype=jnp.int32)[:, None, None]
    outer_y = start_y - 1 + jnp.arange(cells_y + 2, dtype=jnp.int32)[None, :, None]
    extended = build_probes(outer_x, outer_y, coord_z, grid_x, grid_y)
    first = stencil(depth_pad(extended), 1, 0, diagonal) - fault_term(probes)
    smoothed = probes - damping * first / diagonal
    across_smooth = fault_term(smoothed)
    applied = stencil(depth_pad(extend(smoothed)), 1, 0, diagonal) - across_smooth
    scaled = applied / diagonal
    image = stencil(depth_pad(extend(scaled)), 1, 0, diagonal) - fault_term(scaled)
    result = applied - damping * image
    coarse = result.reshape(COLORS, cells_x // 2, 2, cells_y // 2, 2, layers // 2, 2).sum((2, 4, 6))
    return (tentative_value * coarse).reshape(COLORS, cells_x // 2, cells_y // 2 * (layers // 2))


def solution(mesh):
    placed = (
        P(None, "gx", "gy"),
        P("gx", "gy"),
        P("gx", "gy", None),
        P("gx", "gy"),
        P("gx", "gy", None),
    )
    return jax.shard_map(
        per_device, mesh=mesh, in_specs=placed, out_specs=P(None, "gx", "gy"), check_vma=False
    )
```

profile of v0, /device:TPU:17, one launch (start us, length us, event | category | flops | bytes accessed | tf_op | source)
XLA Modules:
  0.0 145.0 jit_solution(12189011419182029264)
XLA Ops:
  2.1 3.5 %collective-permute-start = (f32[13,1,8,128]{3,2,1,0:T(8,128)S(1)}, f32[13,1,8,128]{3,2,1,0:T(8,128)S(1)}, u32[]{:S(2)}, u32[]{:S(2)}) collective-permute-start(f32[13,1,8,128]{3,2,1,0:T(8,128)S(1)} %get-tuple-element.31), channel_id=1, source_target_pairs={{0,4},{4,8},{8,12},{12,16},{16,20},{20,24},{24,28},{28,32},{32,36}... | collective-permute-start | bytes 159752 | tf_op jit(solution)/shard_map/ppermute | solution.py:36
  5.6 11.5 %collective-permute-start.1 = (f32[13,1,8,128]{3,2,1,0:T(8,128)S(1)}, f32[13,1,8,128]{3,2,1,0:T(8,128)S(1)}, u32[]{:S(2)}, u32[]{:S(2)}) collective-permute-start(f32[13,1,8,128]{3,2,1,0:T(8,128)S(1)} %get-tuple-element.32), channel_id=1, source_target_pairs={{4,0},{8,4},{12,8},{16,12},{20,16},{24,20},{28,24},{32,28},{36,32}... | collective-permute-start | bytes 159752 | tf_op jit(solution)/shard_map/ppermute | solution.py:37
  21.7 1.9 %collective-permute-start.4 = (f32[125,512]{0,1:T(8,128)S(1)}, f32[125,512]{0,1:T(8,128)S(1)}, u32[]{:S(2)}, u32[]{:S(2)}) collective-permute-start(f32[125,512]{0,1:T(8,128)S(1)} %select_bitcast_fusion.2), channel_id=1, source_target_pairs={{0,4},{4,0},{8,12},{12,8},{16,20},{20,16},{24,28},{28,24},{32,36},... | collective-permute-start | bytes 768008 | tf_op jit(solution)/shard_map/ppermute | solution.py:45
  26.2 1.9 %fusion.4 = f32[1,2,8,128]{3,0,2,1:T(1,128)S(1)} fusion(s32[2,8,128]{2,1,0:T(8,128)S(1)} %multiply_add_fusion, s32[512]{0:T(512)S(1)} %bitcast.305, f32[1,1,512]{2,1,0:T(1,128)S(1)} %copy-done.25, s32[]{:T(128)} %bitcast.291), kind=kOutput, calls=%fused_computation.36 | convolution fusion | flops 13632512 | bytes 20484 | tf_op jit(solution)/shard_map/dot_general | solution.py:115
  28.1 4.7 %collective-permute-start.2 = (f32[13,4,1,128]{3,2,1,0:T(1,128)S(1)}, f32[13,4,1,128]{3,2,1,0:T(1,128)S(1)}, u32[]{:S(2)}, u32[]{:S(2)}) collective-permute-start(f32[13,4,1,128]{3,2,1,0:T(1,128)S(1)} %get-tuple-element.29), channel_id=1, source_target_pairs={{0,1},{1,2},{2,3},{4,5},{5,6},{6,7},{8,9},{9,10},{10,11},{12,13},{... | collective-permute-start | bytes 79880 | tf_op jit(solution)/shard_map/ppermute | solution.py:36
  32.8 1.9 %collective-permute-start.3 = (f32[13,4,1,128]{3,2,1,0:T(1,128)S(1)}, f32[13,4,1,128]{3,2,1,0:T(1,128)S(1)}, u32[]{:S(2)}, u32[]{:S(2)}) collective-permute-start(f32[13,4,1,128]{3,2,1,0:T(1,128)S(1)} %get-tuple-element.30), channel_id=1, source_target_pairs={{1,0},{2,1},{3,2},{5,4},{6,5},{7,6},{9,8},{10,9},{11,10},{13,12},{... | collective-permute-start | bytes 79880 | tf_op jit(solution)/shard_map/ppermute | solution.py:37
  34.7 3.2 %collective-permute-done.3 = f32[13,4,1,128]{3,2,1,0:T(1,128)S(1)} collective-permute-done((f32[13,4,1,128]{3,2,1,0:T(1,128)S(1)}, f32[13,4,1,128]{3,2,1,0:T(1,128)S(1)}, u32[]{:S(2)}, u32[]{:S(2)}) %collective-permute-start.3) | collective-permute-done | bytes 26656 | tf_op jit(solution)/shard_map/ppermute | solution.py:37
  43.8 1.7 %fusion.3 = f32[125,2048]{1,0:T(8,128)S(1)} fusion(s32[512]{0:T(512)S(1)} %bitcast.306, f32[125,512]{0,1:T(8,128)S(1)} %collective-permute-done.4, f32[512]{0:T(512)S(1)} %fusion.145), kind=kOutput, calls=%fused_computation.35 | convolution fusion | flops 1573976576 | bytes 1284096 | tf_op jit(solution)/shard_map/dot_general | solution.py:137
  45.7 6.5 %divide_subtract_fusion = f32[125,2,8,128]{3,2,1,0:T(8,128)S(1)} fusion(f32[128,16,128]{2,1,0:T(8,128)S(1)} %bitcast.296, f32[125,4,10,128]{3,2,1,0:T(8,128)S(1)} %and_select_fusion, f32[2,8,128]{2,1,0:T(8,128)} %get-tuple-element.71, f32[2,8,128]{2,1,0:T(8,128)} %get-tuple-element.70, f32[2,8,128]{2,1,0:T(8,128)} %get-tuple-element.69, ...), kind=kLoop, calls=%fused_computation.227 | loop fusion | flops 15360000 | bytes 15661584 | tf_op jit(solution)/shard_map/sub | solution.py:150
  53.3 3.6 %collective-permute-start.5 = (f32[125,1,8,128]{3,2,1,0:T(8,128)}, f32[125,1,8,128]{3,2,1,0:T(8,128)S(1)}, u32[]{:S(2)}, u32[]{:S(2)}) collective-permute-start(f32[125,1,8,128]{3,2,1,0:T(8,128)} %get-tuple-element.14), channel_id=1, source_target_pairs={{0,4},{4,8},{8,12},{12,16},{16,20},{20,24},{24,28},{28,32},{32,36}... | collective-permute-start | bytes 1536008 | tf_op jit(solution)/shard_map/ppermute | solution.py:36
  56.9 7.4 %collective-permute-start.6 = (f32[125,1,8,128]{3,2,1,0:T(8,128)}, f32[125,1,8,128]{3,2,1,0:T(8,128)S(1)}, u32[]{:S(2)}, u32[]{:S(2)}) collective-permute-start(f32[125,1,8,128]{3,2,1,0:T(8,128)} %get-tuple-element.15), channel_id=1, source_target_pairs={{4,0},{8,4},{12,8},{16,12},{20,16},{24,20},{28,24},{32,28},{36,32}... | collective-permute-start | bytes 1536008 | tf_op jit(solution)/shard_map/ppermute | solution.py:37
  64.7 1.6 %gather_fusion.1 = f32[512,125]{1,0:T(8,128)} fusion(f32[125,2048]{0,1:T(8,128)S(1)} %bitcast.294, s32[1024]{0:T(1024)S(1)} %pad_clamp_fusion), kind=kCustom, calls=%fused_computation.1.clone | custom fusion | bytes 514048 | tf_op jit(solution)/shard_map/jit(_take)/gather | solution.py:135
  67.6 2.1 %collective-permute-start.9 = (f32[125,512]{0,1:T(8,128)S(1)}, f32[125,512]{0,1:T(8,128)S(1)}, u32[]{:S(2)}, u32[]{:S(2)}) collective-permute-start(f32[125,512]{0,1:T(8,128)S(1)} %select_bitcast_fusion.1), channel_id=1, source_target_pairs={{0,4},{4,0},{8,12},{12,8},{16,20},{20,16},{24,28},{28,24},{32,36},... | collective-permute-start | bytes 768008 | tf_op jit(solution)/shard_map/ppermute | solution.py:45
  69.6 3.3 %collective-permute-done.5 = f32[125,1,8,128]{3,2,1,0:T(8,128)S(1)} collective-permute-done((f32[125,1,8,128]{3,2,1,0:T(8,128)}, f32[125,1,8,128]{3,2,1,0:T(8,128)S(1)}, u32[]{:S(2)}, u32[]{:S(2)}) %collective-permute-start.5) | collective-permute-done | bytes 512032 | tf_op jit(solution)/shard_map/ppermute | solution.py:36
  72.9 1.8 %collective-permute-done.6 = f32[125,1,8,128]{3,2,1,0:T(8,128)S(1)} collective-permute-done((f32[125,1,8,128]{3,2,1,0:T(8,128)}, f32[125,1,8,128]{3,2,1,0:T(8,128)S(1)}, u32[]{:S(2)}, u32[]{:S(2)}) %collective-permute-start.6) | collective-permute-done | bytes 512032 | tf_op jit(solution)/shard_map/ppermute | solution.py:37
  75.1 1.9 %collective-permute-start.7 = (f32[125,4,1,128]{3,2,1,0:T(1,128)S(1)}, f32[125,4,1,128]{3,2,1,0:T(1,128)S(1)}, u32[]{:S(2)}, u32[]{:S(2)}) collective-permute-start(f32[125,4,1,128]{3,2,1,0:T(1,128)S(1)} %get-tuple-element.10), channel_id=1, source_target_pairs={{0,1},{1,2},{2,3},{4,5},{5,6},{6,7},{8,9},{9,10},{10,11},{12,13},{... | collective-permute-start | bytes 768008 | tf_op jit(solution)/shard_map/ppermute | solution.py:36
  77.0 2.6 %collective-permute-start.8 = (f32[125,4,1,128]{3,2,1,0:T(1,128)S(1)}, f32[125,4,1,128]{3,2,1,0:T(1,128)S(1)}, u32[]{:S(2)}, u32[]{:S(2)}) collective-permute-start(f32[125,4,1,128]{3,2,1,0:T(1,128)S(1)} %get-tuple-element.11), channel_id=1, source_target_pairs={{1,0},{2,1},{3,2},{5,4},{6,5},{7,6},{9,8},{10,9},{11,10},{13,12},{... | collective-permute-start | bytes 768008 | tf_op jit(solution)/shard_map/ppermute | solution.py:37
  79.6 1.7 %fusion.2 = f32[125,2048]{1,0:T(8,128)S(1)} fusion(s32[512]{0:T(512)S(1)} %bitcast.307, f32[125,512]{0,1:T(8,128)S(1)} %collective-permute-done.9, f32[512]{0:T(512)S(1)} %copy-done.27), kind=kOutput, calls=%fused_computation.34 | convolution fusion | flops 1573976576 | bytes 1284096 | tf_op jit(solution)/shard_map/dot_general | solution.py:137
  81.5 3.1 %collective-permute-done.8 = f32[125,4,1,128]{3,2,1,0:T(1,128)S(1)} collective-permute-done((f32[125,4,1,128]{3,2,1,0:T(1,128)S(1)}, f32[125,4,1,128]{3,2,1,0:T(1,128)S(1)}, u32[]{:S(2)}, u32[]{:S(2)}) %collective-permute-start.8) | collective-permute-done | bytes 256032 | tf_op jit(solution)/shard_map/ppermute | solution.py:37
  84.6 6.2 %select_maximum_fusion.4 = f32[125,4,10,130]{3,2,1,0:T(8,128)S(1)} fusion(f32[125,4,1,128]{3,2,1,0:T(1,128)S(1)} %collective-permute-done.8, f32[125,4,1,128]{3,2,1,0:T(1,128)S(1)} %collective-permute-done.7, f32[125,1,8,128]{3,2,1,0:T(8,128)S(1)} %collective-permute-done.6, f32[125,2,8,128]{3,2,1,0:T(8,128)S(1)} %divide_subtract_fusion, ...), kind=kLoop, calls=%fused_computation.27 | loop fusion | flops 7800000 | bytes 5160000 | tf_op jit(solution)/shard_map/concatenate | solution.py:38
  91.0 6.9 %broadcast_divide_fusion = (f32[125,2,8,128]{3,2,1,0:T(8,128)S(1)}, f32[125,2,8,128]{3,2,1,0:T(8,128)}) fusion(f32[2,8,128]{2,1,0:T(8,128)S(1)} %copy-done.16, f32[128,16,128]{2,1,0:T(8,128)S(1)} %bitcast.297, f32[125,4,10,130]{3,2,1,0:T(8,128)S(1)} %select_maximum_fusion.4, f32[2,8,128]{2,1,0:T(8,128)S(1)} %copy-done.15, f32[2,8,128]{2,1,0:T(8,128)S(1)} %copy-done.14, ...), kind=kLoop, calls=%fused_computation.233 | loop fusion | flops 19200000 | bytes 24285184 | tf_op jit(solution)/shard_map/div | solution.py:153
  98.9 1.9 %collective-permute-start.10 = (f32[125,1,8,128]{3,2,1,0:T(8,128)}, f32[125,1,8,128]{3,2,1,0:T(8,128)S(1)}, u32[]{:S(2)}, u32[]{:S(2)}) collective-permute-start(f32[125,1,8,128]{3,2,1,0:T(8,128)} %get-tuple-element.12), channel_id=1, source_target_pairs={{0,4},{4,8},{8,12},{12,16},{16,20},{20,24},{24,28},{28,32},{32,36}... | collective-permute-start | bytes 1536008 | tf_op jit(solution)/shard_map/ppermute | solution.py:36
  100.8 9.5 %collective-permute-start.11 = (f32[125,1,8,128]{3,2,1,0:T(8,128)}, f32[125,1,8,128]{3,2,1,0:T(8,128)S(1)}, u32[]{:S(2)}, u32[]{:S(2)}) collective-permute-start(f32[125,1,8,128]{3,2,1,0:T(8,128)} %get-tuple-element.13), channel_id=1, source_target_pairs={{4,0},{8,4},{12,8},{16,12},{20,16},{24,20},{28,24},{32,28},{36,32}... | collective-permute-start | bytes 1536008 | tf_op jit(solution)/shard_map/ppermute | solution.py:37
  113.5 1.9 %collective-permute-start.14 = (f32[125,512]{0,1:T(8,128)S(1)}, f32[125,512]{0,1:T(8,128)S(1)}, u32[]{:S(2)}, u32[]{:S(2)}) collective-permute-start(f32[125,512]{0,1:T(8,128)S(1)} %select_bitcast_fusion), channel_id=1, source_target_pairs={{0,4},{4,0},{8,12},{12,8},{16,20},{20,16},{24,28},{28,24},{32,36},... | collective-permute-start | bytes 768008 | tf_op jit(solution)/shard_map/ppermute | solution.py:45
  115.5 1.7 %collective-permute-done.10 = f32[125,1,8,128]{3,2,1,0:T(8,128)S(1)} collective-permute-done((f32[125,1,8,128]{3,2,1,0:T(8,128)}, f32[125,1,8,128]{3,2,1,0:T(8,128)S(1)}, u32[]{:S(2)}, u32[]{:S(2)}) %collective-permute-start.10) | collective-permute-done | bytes 512032 | tf_op jit(solution)/shard_map/ppermute | solution.py:36
  117.2 1.8 %collective-permute-done.11 = f32[125,1,8,128]{3,2,1,0:T(8,128)S(1)} collective-permute-done((f32[125,1,8,128]{3,2,1,0:T(8,128)}, f32[125,1,8,128]{3,2,1,0:T(8,128)S(1)}, u32[]{:S(2)}, u32[]{:S(2)}) %collective-permute-start.11) | collective-permute-done | bytes 512032 | tf_op jit(solution)/shard_map/ppermute | solution.py:37
  119.3 1.9 %collective-permute-start.12 = (f32[125,4,1,128]{3,2,1,0:T(1,128)S(1)}, f32[125,4,1,128]{3,2,1,0:T(1,128)S(1)}, u32[]{:S(2)}, u32[]{:S(2)}) collective-permute-start(f32[125,4,1,128]{3,2,1,0:T(1,128)S(1)} %get-tuple-element.8), channel_id=1, source_target_pairs={{0,1},{1,2},{2,3},{4,5},{5,6},{6,7},{8,9},{9,10},{10,11},{12,13},{... | collective-permute-start | bytes 768008 | tf_op jit(solution)/shard_map/ppermute | solution.py:36
  121.2 2.6 %collective-permute-start.13 = (f32[125,4,1,128]{3,2,1,0:T(1,128)S(1)}, f32[125,4,1,128]{3,2,1,0:T(1,128)S(1)}, u32[]{:S(2)}, u32[]{:S(2)}) collective-permute-start(f32[125,4,1,128]{3,2,1,0:T(1,128)S(1)} %get-tuple-element.9), channel_id=1, source_target_pairs={{1,0},{2,1},{3,2},{5,4},{6,5},{7,6},{9,8},{10,9},{11,10},{13,12},{... | collective-permute-start | bytes 768008 | tf_op jit(solution)/shard_map/ppermute | solution.py:37
  123.9 1.7 %fusion.1 = f32[125,2048]{1,0:T(8,128)S(1)} fusion(s32[512]{0:T(512)S(1)} %bitcast.308, f32[125,512]{0,1:T(8,128)S(1)} %collective-permute-done.14, f32[512]{0:T(512)S(1)} %copy-done.28), kind=kOutput, calls=%fused_computation.33 | convolution fusion | flops 1573976576 | bytes 1284096 | tf_op jit(solution)/shard_map/dot_general | solution.py:137
  125.8 3.1 %collective-permute-done.13 = f32[125,4,1,128]{3,2,1,0:T(1,128)S(1)} collective-permute-done((f32[125,4,1,128]{3,2,1,0:T(1,128)S(1)}, f32[125,4,1,128]{3,2,1,0:T(1,128)S(1)}, u32[]{:S(2)}, u32[]{:S(2)}) %collective-permute-start.13) | collective-permute-done | bytes 256032 | tf_op jit(solution)/shard_map/ppermute | solution.py:37
  128.8 6.2 %select_maximum_fusion = f32[125,4,10,130]{3,2,1,0:T(8,128)S(1)} fusion(f32[125,4,1,128]{3,2,1,0:T(1,128)S(1)} %collective-permute-done.13, f32[125,4,1,128]{3,2,1,0:T(1,128)S(1)} %collective-permute-done.12, f32[125,1,8,128]{3,2,1,0:T(8,128)S(1)} %collective-permute-done.11, f32[125,2,8,128]{3,2,1,0:T(8,128)S(1)} %get-tuple-element.6, ...), kind=kLoop, calls=%fused_computation.23 | loop fusion | flops 7800000 | bytes 5160000 | tf_op jit(solution)/shard_map/concatenate | solution.py:38
  135.1 7.4 %fusion.57 = f32[125,8,128]{2,1,0:T(8,128)} fusion(f32[125,2,8,128]{3,2,1,0:T(8,128)} %get-tuple-element.7, f32[128,16,128]{2,1,0:T(8,128)S(1)} %bitcast.295, f32[125,4,10,130]{3,2,1,0:T(8,128)S(1)} %select_maximum_fusion, f32[125,4,1,128]{3,2,1,0:T(1,128)} %copy-done, f32[125,1,8,128]{3,2,1,0:T(8,128)S(1)} %collective-permute-done.11, ...), kind=kLoop, calls=%fused_computation.94 | loop fusion | flops 19584000 | bytes 23773184 | tf_op jit(solution)/shard_map/reduce_sum | solution.py:156
  (152 shorter events, 24.8 us)
Async XLA Ops:
  0.0 26.1 %copy-start.21 = (s32[1,1,512]{2,1,0:T(1,128)S(1)}, s32[1,1,512]{2,1,0:T(1,128)}, u32[]{:S(2)}) copy-start(s32[1,1,512]{2,1,0:T(1,128)} %param.9) | copy-start | bytes 6148
  0.0 26.2 %copy-start.25 = (f32[1,1,512]{2,1,0:T(1,128)S(1)}, f32[1,1,512]{2,1,0:T(1,128)}, u32[]{:S(2)}) copy-start(f32[1,1,512]{2,1,0:T(1,128)} %param.11) | copy-start | bytes 6148
  0.0 43.1 %copy-start.24 = (f32[2,1024]{1,0:T(2,128)S(1)}, f32[2,1024]{1,0:T(2,128)}, u32[]{:S(2)}) copy-start(f32[2,1024]{1,0:T(2,128)} %param.8) | copy-start | bytes 24580
  1.1 44.4 %copy-start.17 = (pred[2,8]{1,0:T(4,128)(4,1)}, pred[2,8]{1,0:T(4,128)(4,1)S(1)}, u32[]{:S(2)}) copy-start(pred[2,8]{1,0:T(4,128)(4,1)S(1)} %get-tuple-element.77) | copy-start | bytes 52
  2.1 26.0 %collective-permute-start = (f32[13,1,8,128]{3,2,1,0:T(8,128)S(1)}, f32[13,1,8,128]{3,2,1,0:T(8,128)S(1)}, u32[]{:S(2)}, u32[]{:S(2)}) collective-permute-start(f32[13,1,8,128]{3,2,1,0:T(8,128)S(1)} %get-tuple-element.31), channel_id=1, source_target_pairs={{0,4},{4,8},{8,12},{12,16},{16,20},{20,24},{24,28},{28,32},{32,36}... | collective-permute-start | bytes 159752 | tf_op jit(solution)/shard_map/ppermute | solution.py:36
  5.6 22.5 %collective-permute-start.1 = (f32[13,1,8,128]{3,2,1,0:T(8,128)S(1)}, f32[13,1,8,128]{3,2,1,0:T(8,128)S(1)}, u32[]{:S(2)}, u32[]{:S(2)}) collective-permute-start(f32[13,1,8,128]{3,2,1,0:T(8,128)S(1)} %get-tuple-element.32), channel_id=1, source_target_pairs={{4,0},{8,4},{12,8},{16,12},{20,16},{24,20},{28,24},{32,28},{36,32}... | collective-permute-start | bytes 159752 | tf_op jit(solution)/shard_map/ppermute | solution.py:37
  21.7 22.1 %collective-permute-start.4 = (f32[125,512]{0,1:T(8,128)S(1)}, f32[125,512]{0,1:T(8,128)S(1)}, u32[]{:S(2)}, u32[]{:S(2)}) collective-permute-start(f32[125,512]{0,1:T(8,128)S(1)} %select_bitcast_fusion.2), channel_id=1, source_target_pairs={{0,4},{4,0},{8,12},{12,8},{16,20},{20,16},{24,28},{28,24},{32,36},... | collective-permute-start | bytes 768008 | tf_op jit(solution)/shard_map/ppermute | solution.py:45
  28.1 6.6 %collective-permute-start.2 = (f32[13,4,1,128]{3,2,1,0:T(1,128)S(1)}, f32[13,4,1,128]{3,2,1,0:T(1,128)S(1)}, u32[]{:S(2)}, u32[]{:S(2)}) collective-permute-start(f32[13,4,1,128]{3,2,1,0:T(1,128)S(1)} %get-tuple-element.29), channel_id=1, source_target_pairs={{0,1},{1,2},{2,3},{4,5},{5,6},{6,7},{8,9},{9,10},{10,11},{12,13},{... | collective-permute-start | bytes 79880 | tf_op jit(solution)/shard_map/ppermute | solution.py:36
  32.8 5.2 %collective-permute-start.3 = (f32[13,4,1,128]{3,2,1,0:T(1,128)S(1)}, f32[13,4,1,128]{3,2,1,0:T(1,128)S(1)}, u32[]{:S(2)}, u32[]{:S(2)}) collective-permute-start(f32[13,4,1,128]{3,2,1,0:T(1,128)S(1)} %get-tuple-element.30), channel_id=1, source_target_pairs={{1,0},{2,1},{3,2},{5,4},{6,5},{7,6},{9,8},{10,9},{11,10},{13,12},{... | collective-permute-start | bytes 79880 | tf_op jit(solution)/shard_map/ppermute | solution.py:37
  52.2 27.4 %copy-start.22 = (s32[1,1,512]{2,1,0:T(1,128)S(1)}, s32[1,1,512]{2,1,0:T(1,128)}, u32[]{:S(2)}) copy-start(s32[1,1,512]{2,1,0:T(1,128)} %param.9) | copy-start | bytes 6148
  52.2 27.4 %copy-start.27 = (f32[512]{0:T(512)S(1)}, f32[512]{0:T(512)}, u32[]{:S(2)}) copy-start(f32[512]{0:T(512)} %copy-done.26) | copy-start | bytes 6148
  53.3 19.7 %collective-permute-start.5 = (f32[125,1,8,128]{3,2,1,0:T(8,128)}, f32[125,1,8,128]{3,2,1,0:T(8,128)S(1)}, u32[]{:S(2)}, u32[]{:S(2)}) collective-permute-start(f32[125,1,8,128]{3,2,1,0:T(8,128)} %get-tuple-element.14), channel_id=1, source_target_pairs={{0,4},{4,8},{8,12},{12,16},{16,20},{20,24},{24,28},{28,32},{32,36}... | collective-permute-start | bytes 1536008 | tf_op jit(solution)/shard_map/ppermute | solution.py:36
  56.9 17.8 %collective-permute-start.6 = (f32[125,1,8,128]{3,2,1,0:T(8,128)}, f32[125,1,8,128]{3,2,1,0:T(8,128)S(1)}, u32[]{:S(2)}, u32[]{:S(2)}) collective-permute-start(f32[125,1,8,128]{3,2,1,0:T(8,128)} %get-tuple-element.15), channel_id=1, source_target_pairs={{4,0},{8,4},{12,8},{16,12},{20,16},{24,20},{28,24},{32,28},{36,32}... | collective-permute-start | bytes 1536008 | tf_op jit(solution)/shard_map/ppermute | solution.py:37
  67.4 23.4 %copy-start.4 = (f32[2,8,128]{2,1,0:T(8,128)S(1)}, f32[2,8,128]{2,1,0:T(8,128)}, u32[]{:S(2)}) copy-start(f32[2,8,128]{2,1,0:T(8,128)} %get-tuple-element.60) | copy-start | bytes 24580
  67.4 23.4 %copy-start.5 = (f32[2,8,128]{2,1,0:T(8,128)S(1)}, f32[2,8,128]{2,1,0:T(8,128)}, u32[]{:S(2)}) copy-start(f32[2,8,128]{2,1,0:T(8,128)} %get-tuple-element.61) | copy-start | bytes 24580
  67.5 23.4 %copy-start.6 = (f32[2,8,128]{2,1,0:T(8,128)S(1)}, f32[2,8,128]{2,1,0:T(8,128)}, u32[]{:S(2)}) copy-start(f32[2,8,128]{2,1,0:T(8,128)} %get-tuple-element.62) | copy-start | bytes 24580
  67.5 23.4 %copy-start.7 = (f32[2,8,128]{2,1,0:T(8,128)S(1)}, f32[2,8,128]{2,1,0:T(8,128)}, u32[]{:S(2)}) copy-start(f32[2,8,128]{2,1,0:T(8,128)} %get-tuple-element.63) | copy-start | bytes 24580
  67.5 23.4 %copy-start.8 = (f32[2,8,128]{2,1,0:T(8,128)S(1)}, f32[2,8,128]{2,1,0:T(8,128)}, u32[]{:S(2)}) copy-start(f32[2,8,128]{2,1,0:T(8,128)} %get-tuple-element.64) | copy-start | bytes 24580
  67.5 23.4 %copy-start.9 = (f32[2,8,128]{2,1,0:T(8,128)S(1)}, f32[2,8,128]{2,1,0:T(8,128)}, u32[]{:S(2)}) copy-start(f32[2,8,128]{2,1,0:T(8,128)} %get-tuple-element.65) | copy-start | bytes 24580
  67.5 23.4 %copy-start.10 = (f32[2,8,128]{2,1,0:T(8,128)S(1)}, f32[2,8,128]{2,1,0:T(8,128)}, u32[]{:S(2)}) copy-start(f32[2,8,128]{2,1,0:T(8,128)} %get-tuple-element.66) | copy-start | bytes 24580
  67.5 23.4 %copy-start.11 = (f32[2,8,128]{2,1,0:T(8,128)S(1)}, f32[2,8,128]{2,1,0:T(8,128)}, u32[]{:S(2)}) copy-start(f32[2,8,128]{2,1,0:T(8,128)} %get-tuple-element.67) | copy-start | bytes 24580
  67.5 23.4 %copy-start.12 = (f32[2,8,128]{2,1,0:T(8,128)S(1)}, f32[2,8,128]{2,1,0:T(8,128)}, u32[]{:S(2)}) copy-start(f32[2,8,128]{2,1,0:T(8,128)} %get-tuple-element.68) | copy-start | bytes 24580
  67.6 12.0 %collective-permute-start.9 = (f32[125,512]{0,1:T(8,128)S(1)}, f32[125,512]{0,1:T(8,128)S(1)}, u32[]{:S(2)}, u32[]{:S(2)}) collective-permute-start(f32[125,512]{0,1:T(8,128)S(1)} %select_bitcast_fusion.1), channel_id=1, source_target_pairs={{0,4},{4,0},{8,12},{12,8},{16,20},{20,16},{24,28},{28,24},{32,36},... | collective-permute-start | bytes 768008 | tf_op jit(solution)/shard_map/ppermute | solution.py:45
  75.1 6.4 %collective-permute-start.7 = (f32[125,4,1,128]{3,2,1,0:T(1,128)S(1)}, f32[125,4,1,128]{3,2,1,0:T(1,128)S(1)}, u32[]{:S(2)}, u32[]{:S(2)}) collective-permute-start(f32[125,4,1,128]{3,2,1,0:T(1,128)S(1)} %get-tuple-element.10), channel_id=1, source_target_pairs={{0,1},{1,2},{2,3},{4,5},{5,6},{6,7},{8,9},{9,10},{10,11},{12,13},{... | collective-permute-start | bytes 768008 | tf_op jit(solution)/shard_map/ppermute | solution.py:36
  77.0 7.6 %collective-permute-start.8 = (f32[125,4,1,128]{3,2,1,0:T(1,128)S(1)}, f32[125,4,1,128]{3,2,1,0:T(1,128)S(1)}, u32[]{:S(2)}, u32[]{:S(2)}) collective-permute-start(f32[125,4,1,128]{3,2,1,0:T(1,128)S(1)} %get-tuple-element.11), channel_id=1, source_target_pairs={{1,0},{2,1},{3,2},{5,4},{6,5},{7,6},{9,8},{10,9},{11,10},{13,12},{... | collective-permute-start | bytes 768008 | tf_op jit(solution)/shard_map/ppermute | solution.py:37
  97.9 26.0 %copy-start.23 = (s32[1,1,512]{2,1,0:T(1,128)S(1)}, s32[1,1,512]{2,1,0:T(1,128)}, u32[]{:S(2)}) copy-start(s32[1,1,512]{2,1,0:T(1,128)} %param.9) | copy-start | bytes 6148
  97.9 26.0 %copy-start.28 = (f32[512]{0:T(512)S(1)}, f32[512]{0:T(512)}, u32[]{:S(2)}) copy-start(f32[512]{0:T(512)} %copy-done.26) | copy-start | bytes 6148
  98.9 18.2 %collective-permute-start.10 = (f32[125,1,8,128]{3,2,1,0:T(8,128)}, f32[125,1,8,128]{3,2,1,0:T(8,128)S(1)}, u32[]{:S(2)}, u32[]{:S(2)}) collective-permute-start(f32[125,1,8,128]{3,2,1,0:T(8,128)} %get-tuple-element.12), channel_id=1, source_target_pairs={{0,4},{4,8},{8,12},{12,16},{16,20},{20,24},{24,28},{28,32},{32,36}... | collective-permute-start | bytes 1536008 | tf_op jit(solution)/shard_map/ppermute | solution.py:36
  100.8 18.1 %collective-permute-start.11 = (f32[125,1,8,128]{3,2,1,0:T(8,128)}, f32[125,1,8,128]{3,2,1,0:T(8,128)S(1)}, u32[]{:S(2)}, u32[]{:S(2)}) collective-permute-start(f32[125,1,8,128]{3,2,1,0:T(8,128)} %get-tuple-element.13), channel_id=1, source_target_pairs={{4,0},{8,4},{12,8},{16,12},{20,16},{24,20},{28,24},{32,28},{36,32}... | collective-permute-start | bytes 1536008 | tf_op jit(solution)/shard_map/ppermute | solution.py:37
  113.5 10.3 %collective-permute-start.14 = (f32[125,512]{0,1:T(8,128)S(1)}, f32[125,512]{0,1:T(8,128)S(1)}, u32[]{:S(2)}, u32[]{:S(2)}) collective-permute-start(f32[125,512]{0,1:T(8,128)S(1)} %select_bitcast_fusion), channel_id=1, source_target_pairs={{0,4},{4,0},{8,12},{12,8},{16,20},{20,16},{24,28},{28,24},{32,36},... | collective-permute-start | bytes 768008 | tf_op jit(solution)/shard_map/ppermute | solution.py:45
  119.3 6.5 %collective-permute-start.12 = (f32[125,4,1,128]{3,2,1,0:T(1,128)S(1)}, f32[125,4,1,128]{3,2,1,0:T(1,128)S(1)}, u32[]{:S(2)}, u32[]{:S(2)}) collective-permute-start(f32[125,4,1,128]{3,2,1,0:T(1,128)S(1)} %get-tuple-element.8), channel_id=1, source_target_pairs={{0,1},{1,2},{2,3},{4,5},{5,6},{6,7},{8,9},{9,10},{10,11},{12,13},{... | collective-permute-start | bytes 768008 | tf_op jit(solution)/shard_map/ppermute | solution.py:36
  121.2 7.6 %collective-permute-start.13 = (f32[125,4,1,128]{3,2,1,0:T(1,128)S(1)}, f32[125,4,1,128]{3,2,1,0:T(1,128)S(1)}, u32[]{:S(2)}, u32[]{:S(2)}) collective-permute-start(f32[125,4,1,128]{3,2,1,0:T(1,128)S(1)} %get-tuple-element.9), channel_id=1, source_target_pairs={{1,0},{2,1},{3,2},{5,4},{6,5},{7,6},{9,8},{10,9},{11,10},{13,12},{... | collective-permute-start | bytes 768008 | tf_op jit(solution)/shard_map/ppermute | solution.py:37
  (12 other events, 177.4 us)
where the time goes:
time: 146 us; the launch traced here: 145 us
  starting transfers between devices  59 us (40%)
  other arithmetic  43.4 us (30%)
  waiting for transfers between devices  17.9 us (12%)
  local copies, waits for them, and re-layouts  16.2 us (11%)
  matrix products  6.88 us (5%)
  between operations  1.55 us (1%)
    ppermute x6, starting transfers between devices, with_halo(): after = lax.ppermute(leading, axis, down)  35.5 us
    ppermute x6, starting transfers between devices, with_halo(): before = lax.ppermute(last, axis, up)  17.6 us
    concatenate x3, other arithmetic, with_halo(): value = jnp.concatenate([before, value, after], axis=dim)  12.9 us
    ppermute x6, waiting for transfers between devices, with_halo(): after = lax.ppermute(leading, axis, down)  12.9 us
    reduce_sum x2, other arithmetic, per_device(): result.reshape(COLORS, cells_x // 2, 2, cells_y // 2, 2, layers // 2, 2)  7.85 us
    div x1, other arithmetic, per_device(): scaled = applied / diagonal  6.86 us
    sub x1, other arithmetic, per_device(): smoothed = probes - damping * first / diagonal  6.46 us
    ppermute x3, starting transfers between devices, from_partner(): return lax.ppermute(value, axis, pairs)  5.89 us
  transfers between devices with their start and end apart: 15, of which 7 were waited for; matrix products, arithmetic and copies ran while one was open for 17% of the time, Pallas kernels for 0%

commit v1 on v0

v1 whole, which is shorter than its diff:
```python
import jax
import jax.numpy as jnp
from jax import lax
from jax.experimental import pallas as pl
from jax.experimental.pallas import tpu as pltpu
from jax.sharding import PartitionSpec as P

FORWARD = (
    (0, 0, 1),
    (0, 1, -1),
    (0, 1, 0),
    (0, 1, 1),
    (1, -1, -1),
    (1, -1, 0),
    (1, -1, 1),
    (1, 0, -1),
    (1, 0, 0),
    (1, 0, 1),
    (1, 1, -1),
    (1, 1, 0),
    (1, 1, 1),
)
damping = 2.0 / 3.0
tent = 0.35355339059327373
F32 = jnp.float32


def kid(dx, dy, dz):
    return (dx + 1) * 9 + (dy + 1) * 3 + dz + 1


def body(meta, c_ref, f_ref, out_ref, kf, inv_ref, fd, pat, bands, fp, gs, s3, ap, b3, acc_ref):
    gx = meta[0]
    gy = meta[1]
    odd_dev = lax.rem(gx, 2)
    zl = lax.broadcasted_iota(jnp.int32, (16, 128), 1)
    yi = lax.broadcasted_iota(jnp.int32, (16, 128), 0)
    yg = gy * 8 + yi - 3
    y_odd = lax.rem(yi, 2) == 0

    e8 = lax.broadcasted_iota(jnp.int32, (8, 128), 0)
    z8 = lax.broadcasted_iota(jnp.int32, (8, 128), 1)
    for d in range(17):
        col = lax.rem(lax.shift_right_logical(z8 + (d - 8 + 160), 1), 5)
        pat[d] = jnp.where(col == e8, F32(1.0), F32(0.0))

    wsum = [jnp.zeros((16, 128), F32) for _ in range(6)]
    for o, (dx, dy, dz) in enumerate(FORWARD):
        ok = (yg + dy >= 0) & (yg + dy < 32) & (zl + dz >= 0) & (zl + dz < 128)
        for x in range(-3, 4):
            if dx == 0 and x == -3:
                continue
            m = jnp.where(ok, c_ref[o, x + 3], F32(0.0))
            if dx:
                m = m * (2 * gx + x + 1 < 256).astype(F32)
            if x >= -2:
                kf[kid(dx, dy, dz), x + 2] = -m
                wsum[x + 2] = wsum[x + 2] + m
            xb = x + dx
            if -2 <= xb <= 3:
                b = m
                if dy:
                    b = pltpu.roll(b, dy % 16, 0)
                if dz:
                    b = pltpu.roll(b, dz % 128, 1)
                kf[kid(-dx, -dy, -dz), xb + 2] = -b
                wsum[xb + 2] = wsum[xb + 2] + b

    x_own = 1 - odd_dev
    x_par = 2 - 3 * odd_dev
    x_oth = 5 * odd_dev - 2
    sides = ((0, 1, 2), (1, 0, 2), (3, 4, 5))
    d24 = lax.broadcasted_iota(jnp.int32, (24, 512), 0) - 8
    for dev, (ylo, ny, yout) in enumerate(((6, 2, 0), (0, 8, 2), (0, 2, 10))):
        for side, (own, par, tr) in enumerate(sides):
            co = f_ref[dev, own : own + 1].astype(jnp.int32) & 1023
            cp = f_ref[dev, par : par + 1].astype(jnp.int32) & 1023
            t = f_ref[dev, tr : tr + 1]
            delta = (cp & 127) - (co & 127)
            bt = jnp.where(d24 == delta, t, F32(0.0))
            hi = bt.astype(jnp.bfloat16)
            r1 = bt - hi.astype(F32)
            mid = r1.astype(jnp.bfloat16)
            low = (r1 - mid.astype(F32)).astype(jnp.bfloat16)
            rows = lax.broadcasted_iota(jnp.int32, (ny * 128, 512), 0) + ylo * 128
            hot = jnp.where(rows == co, F32(1.0), F32(0.0)).astype(jnp.bfloat16)
            dims = (((1,), (1,)), ((), ()))
            got = lax.dot_general(hi, hot, dims, preferred_element_type=F32)
            got = got + lax.dot_general(mid, hot, dims, preferred_element_type=F32)
            got = got + lax.dot_general(low, hot, dims, preferred_element_type=F32)
            for y in range(ny):
                bands[side, yout + y] = got[:, y * 128 : (y + 1) * 128]

    fd[...] = jnp.zeros((6, 16, 128), F32)
    for side, xs in enumerate((x_own, x_par, x_oth)):
        for y in range(12):
            tile = jnp.zeros((8, 128), F32)
            for d in range(17):
                tile = tile + bands[side, y, d : d + 1, :] * pat[d]
            fp[side, y] = tile
            fd[xs + 2, y + 1 : y + 2, :] = jnp.sum(tile, axis=0, keepdims=True)

    for x in range(-2, 4):
        diag = c_ref[13, x + 3] + wsum[x + 2] + fd[x + 2]
        inv = jnp.where(diag > 0.0, 1.0 / diag, F32(0.0))
        kf[13, x + 2] = diag
        inv_ref[x + 2] = inv
        for dz in (-1, 0, 1):
            low, high = [], []
            for dx in (-1, 0, 1):
                mid = kf[kid(dx, 0, dz), x + 2]
                low.append(kf[kid(dx, -1, dz), x + 2] + jnp.where(y_odd, mid, F32(0.0)))
                high.append(kf[kid(dx, 1, dz), x + 2] + jnp.where(y_odd, F32(0.0), mid))
            for ry, part in enumerate((low, high)):
                if x % 2:
                    pair = (part[0] + part[1], part[2])
                else:
                    pair = (part[0], part[1] + part[2])
                for rx, total in enumerate(pair):
                    g = inv * total * F32(-damping * tent)
                    if dz == 0 and rx == (0 if x % 2 else 1):
                        mine = y_odd if ry == 0 else jnp.logical_not(y_odd)
                        g = g + jnp.where(mine, F32(tent), F32(0.0))
                    gs[x + 2, rx * 2 + ry, dz + 1] = g

    def smooth(y, carry):
        for x in range(6):
            for r in range(4):
                tile = gs[x, r, 0, pl.ds(y + 1, 1), :] * pat[7]
                tile = tile + gs[x, r, 1, pl.ds(y + 1, 1), :] * pat[8]
                tile = tile + gs[x, r, 2, pl.ds(y + 1, 1), :] * pat[9]
                s3[1, x, y, r] = tile
        ry = 1 - lax.rem(y, 2)
        for side, xs in enumerate((x_own, x_par, x_oth)):
            rx = xs & 1
            iv = inv_ref[xs + 2, pl.ds(y + 1, 1), :] * F32(damping * tent)
            s3[1, xs + 2, y, rx * 2 + ry] += iv * fp[side, y]
        for x in range(6):
            for r in range(4):
                tile = s3[1, x, y, r]
                s3[0, x, y, r] = pltpu.roll(tile, 1, 1)
                s3[2, x, y, r] = pltpu.roll(tile, 127, 1)
        return carry

    lax.fori_loop(0, 12, smooth, 0)

    def apply_pair(t, carry):
        for x in range(-1, 3):
            for p in range(2):
                y = p - 1
                acc = [None] * 9
                for dx in (-1, 0, 1):
                    for dy in (-1, 0, 1):
                        xn, yn = x + dx, y + dy
                        bx = (xn - 1) // 2 - (x // 2 - 1)
                        by = (yn - 1) // 2 - (y // 2 - 1)
                        for dz in (-1, 0, 1):
                            row = kf[kid(dx, dy, dz), x + 2, pl.ds(2 * t + y + 3, 1), :]
                            for rx in range(2):
                                for ry in range(2):
                                    q = (bx + rx) * 3 + by + ry
                                    v = row * s3[dz + 1, xn + 2, 2 * t + yn + 2, rx * 2 + ry]
                                    acc[q] = v if acc[q] is None else acc[q] + v
                for q in range(9):
                    ap[x + 1, 2 * t + y + 1, q] = acc[q]
        return carry

    lax.fori_loop(0, 5, apply_pair, 0)

    def apply_fault(n, carry):
        y = n - 1
        y_is_odd = y & 1
        for side, (xs, xn) in enumerate(((x_own, x_par), (x_par, x_own))):
            for rx in range(2):
                for ry in range(2):
                    tile = s3[1, xn + 2, n + 1, rx * 2 + ry]
                    total = jnp.zeros((8, 128), F32)
                    for d in range(17):
                        row = bands[side, n + 1, d : d + 1, :]
                        total = total + row * pltpu.roll(tile, (8 - d) % 128, 1)
                    q = ((xs & 1) + rx) * 3 + y_is_odd + ry
                    ap[xs + 1, n, q] -= total
        for x in range(4):
            iv = inv_ref[x + 1, pl.ds(n + 2, 1), :]
            for q in range(9):
                tile = ap[x, n, q] * iv
                b3[1, x, n, q] = tile
                b3[0, x, n, q] = pltpu.roll(tile, 1, 1)
                b3[2, x, n, q] = pltpu.roll(tile, 127, 1)
        return carry

    lax.fori_loop(0, 10, apply_fault, 0)

    pz = lax.broadcasted_iota(jnp.int32, (128, 64), 0)
    pc = lax.broadcasted_iota(jnp.int32, (128, 64), 1)
    pick = jnp.where(lax.shift_right_logical(pz, 1) == pc, F32(tent), F32(0.0))

    def restrict(yc, carry):
        acc = [None] * 25
        for xn in range(-1, 3):
            for yn in range(-1, 3):
                bx, by = xn // 2 + 1, yn // 2 + 1
                for dz in (-1, 0, 1):
                    row = None
                    for x in (0, 1):
                        for y in (0, 1):
                            if abs(xn - x) <= 1 and abs(yn - y) <= 1:
                                k = kf[kid(xn - x, yn - y, dz), x + 2, pl.ds(2 * yc + y + 3, 1), :]
                                row = k if row is None else row + k
                    row = row * F32(-damping)
                    if dz == 0 and xn in (0, 1) and yn in (0, 1):
                        row = row + kf[13, xn + 2, pl.ds(2 * yc + yn + 3, 1), :]
                    for rx in range(3):
                        for ry in range(3):
                            q = (bx + rx) * 5 + by + ry
                            v = row * b3[dz + 1, xn + 1, 2 * yc + yn + 1, rx * 3 + ry]
                            acc[q] = v if acc[q] is None else acc[q] + v
        for q in range(25):
            acc_ref[q // 5, q % 5] = acc[q]
        far = lax.shift_right_arithmetic(x_par, 1) + 1
        for rx in range(3):
            for ry in range(3):
                total = jnp.zeros((8, 128), F32)
                for y in range(2):
                    tile = b3[1, x_par + 1, 2 * yc + y + 1, rx * 3 + ry]
                    for d in range(17):
                        row = bands[0, 2 * yc + y + 2, d : d + 1, :]
                        total = total + row * pltpu.roll(tile, (8 - d) % 128, 1)
                acc_ref[far + rx, 1 + ry] += total * F32(damping)
        got = jnp.dot(
            acc_ref[...].reshape(200, 128),
            pick,
            precision=lax.Precision.HIGHEST,
            preferred_element_type=F32,
        )
        for rx in range(5):
            a = lax.rem(gx + rx + 3, 5)
            for ry in range(5):
                b = lax.rem(gy * 4 + yc + ry + 3, 5)
                q = (rx * 5 + ry) * 8
                out_ref[a, b, yc] = got[q : q + 8]
        return carry

    lax.fori_loop(0, 4, restrict, 0)


def per_device(trans, storage, fault_cells, fault_count, fault_trans):
    gx = lax.axis_index("gx")
    gy = lax.axis_index("gy")
    n_gx = lax.axis_size("gx")
    n_gy = lax.axis_size("gy")
    slots = jnp.arange(512, dtype=jnp.int32)
    live = jnp.where(slots < fault_count.reshape(()), fault_trans.reshape(-1), F32(0.0))
    cells = fault_cells.reshape(-1).astype(F32)
    fault = jnp.concatenate([cells.reshape(4, 128), live.reshape(4, 128)], axis=0)
    core = jnp.concatenate(
        [trans.reshape(13, 2, 8, 128), storage.reshape(1, 2, 8, 128)], axis=0
    )

    def shift(value, axis, size, by):
        pairs = [(i, i + by) for i in range(size) if 0 <= i + by < size]
        return lax.ppermute(value, axis, pairs)

    packed = jnp.concatenate([core.reshape(224, 128), fault], axis=0)
    left = shift(packed, "gx", n_gx, 1)
    right = shift(packed, "gx", n_gx, -1)
    second = jnp.concatenate([core[4:13, 1].reshape(72, 128), fault], axis=0)
    left2 = shift(second, "gx", n_gx, 2)
    right2 = shift(fault, "gx", n_gx, -2)
    far = jnp.concatenate(
        [
            jnp.zeros((4, 1, 8, 128), F32),
            left2[:72].reshape(9, 1, 8, 128),
            jnp.zeros((1, 1, 8, 128), F32),
        ],
        axis=0,
    )
    wide = jnp.concatenate(
        [far, left[:224].reshape(14, 2, 8, 128), core, right[:224].reshape(14, 2, 8, 128)], axis=1
    )
    even = lax.rem(gx, 2) == 0
    partner = jnp.where(even, right[224:228], left[224:228])
    other = jnp.where(even, left[224:], right[224:])
    beyond = jnp.where(even, left2[72:76], right2[:4])
    faults = jnp.concatenate([fault[:4], partner, fault[4:], other[:4], beyond, other[4:]], axis=0)
    up = jnp.concatenate([wide[:, :, 5:].reshape(294, 128), faults], axis=0)
    down = jnp.concatenate([wide[:, :, :3].reshape(294, 128), faults], axis=0)
    below = shift(up, "gy", n_gy, 1)
    above = shift(down, "gy", n_gy, -1)
    full = jnp.concatenate(
        [
            below[:294].reshape(14, 7, 3, 128),
            wide,
            above[:294].reshape(14, 7, 3, 128),
            jnp.zeros((14, 7, 2, 128), F32),
        ],
        axis=2,
    )
    slots3 = jnp.stack([below[294:], faults, above[294:]]).reshape(3, 6, 512)
    meta = jnp.stack([gx, gy]).astype(jnp.int32)
    vm = pl.BlockSpec(memory_space=pltpu.VMEM)
    out = pl.pallas_call(
        body,
        out_shape=jax.ShapeDtypeStruct((5, 5, 4, 8, 64), F32),
        in_specs=[pl.BlockSpec(memory_space=pltpu.SMEM), vm, vm],
        out_specs=vm,
        scratch_shapes=[
            pltpu.VMEM((27, 6, 16, 128), F32),
            pltpu.VMEM((6, 16, 128), F32),
            pltpu.VMEM((6, 16, 128), F32),
            pltpu.VMEM((17, 8, 128), F32),
            pltpu.VMEM((3, 12, 24, 128), F32),
            pltpu.VMEM((3, 12, 8, 128), F32),
            pltpu.VMEM((6, 4, 3, 16, 128), F32),
            pltpu.VMEM((3, 6, 12, 4, 8, 128), F32),
            pltpu.VMEM((4, 10, 9, 8, 128), F32),
            pltpu.VMEM((3, 4, 10, 9, 8, 128), F32),
            pltpu.VMEM((5, 5, 8, 128), F32),
        ],
        compiler_params=pltpu.CompilerParams(vmem_limit_bytes=48 * 1024 * 1024),
    )(meta, full, slots3)
    return out[:, :, :, :5].transpose(0, 1, 3, 2, 4).reshape(125, 1, 256)


def solution(mesh):
    placed = (
        P(None, "gx", "gy"),
        P("gx", "gy"),
        P("gx", "gy", None),
        P("gx", "gy"),
        P("gx", "gy", None),
    )
    return jax.shard_map(
        per_device, mesh=mesh, in_specs=placed, out_specs=P(None, "gx", "gy"), check_vma=False
    )
```

time: 146 us -> 58.9 us (0.40)
  the two profiles are of different devices: /device:TPU:17 before, /device:TPU:24 now
where the time goes in v1:
time: 58.9 us; the launch traced here: 58.6 us
  starting transfers between devices  33 us (56%)
  Pallas kernels  14.6 us (25%)
  waiting for transfers between devices  5.18 us (9%)
  local copies, waits for them, and re-layouts  3.85 us (7%)
  other arithmetic  1.03 us (2%)
  between operations  0.94 us (2%)
    ppermute x6, starting transfers between devices, shift(): return lax.ppermute(value, axis, pairs)  33 us
    pallas_call x1, Pallas kernels, per_device(): pl.pallas_call(body, out_shape=jax.ShapeDtypeStruct((5, 5, 4, 8, 64), F32...  14.6 us
    ppermute x6, waiting for transfers between devices, shift(): return lax.ppermute(value, axis, pairs)  5.18 us
  transfers between devices with their start and end apart: 6, of which 3 were waited for; matrix products, arithmetic and copies ran while one was open for 1% of the time, Pallas kernels for 0%

profile of v1, /device:TPU:24, one launch (start us, length us, event | category | flops | bytes accessed | tf_op | source)
XLA Modules:
  0.0 58.6 jit_solution(2787432623000369875)
XLA Ops:
  0.7 0.7 %convert_element_type.7 = f32[1,1,512]{2,1,0:T(1,128)S(1)} convert(s32[1,1,512]{2,1,0:T(1,128)} %param.7) | non-fusion elementwise | flops 512 | bytes 4096 | tf_op jit(solution)/shard_map/convert_element_type | solution.py:254
  1.3 1.0 %reshape.53 = f32[13,2,8,128]{3,2,1,0:T(8,128)S(1)} reshape(f32[13,2,1024]{2,1,0:T(2,128)} %param.5) | data formatting | bytes 212992 | tf_op jit(solution)/shard_map/reshape | solution.py:257
  2.3 0.0 copy-start.1
  2.4 0.0 copy-start
  2.4 0.6 %copy-done.1 = f32[1,1,512]{2,1,0:T(1,128)S(1)} copy-done((f32[1,1,512]{2,1,0:T(1,128)S(1)}, f32[1,1,512]{2,1,0:T(1,128)}, u32[]{:S(2)}) %copy-start.1) | copy-done | bytes 2072
  3.0 0.0 copy-done
  3.1 14.3 %collective-permute-start.2 = (f32[232,128]{1,0:T(8,128)S(1)}, f32[232,128]{1,0:T(8,128)S(1)}, u32[]{:S(2)}, u32[]{:S(2)}) collective-permute-start(f32[232,128]{1,0:T(8,128)S(1)} %pad_maximum_fusion.1), channel_id=1, source_target_pairs={{4,0},{8,4},{12,8},{16,12},{20,16},{24,20},{28,24},{32,28},{36,32}... | collective-permute-start | bytes 356360 | tf_op jit(solution)/shard_map/ppermute | solution.py:262
  17.3 1.9 %collective-permute-start.1 = (f32[232,128]{1,0:T(8,128)S(1)}, f32[232,128]{1,0:T(8,128)S(1)}, u32[]{:S(2)}, u32[]{:S(2)}) collective-permute-start(f32[232,128]{1,0:T(8,128)S(1)} %pad_maximum_fusion.1), channel_id=1, source_target_pairs={{0,4},{4,8},{8,12},{12,16},{16,20},{20,24},{24,28},{28,32},{32,36}... | collective-permute-start | bytes 356360 | tf_op jit(solution)/shard_map/ppermute | solution.py:262
  19.3 1.9 %collective-permute-start = (f32[80,128]{1,0:T(8,128)S(1)}, f32[80,128]{1,0:T(8,128)S(1)}, u32[]{:S(2)}, u32[]{:S(2)}) collective-permute-start(f32[80,128]{1,0:T(8,128)S(1)} %pad_maximum_fusion.3), channel_id=1, source_target_pairs={{0,8},{4,12},{8,16},{12,20},{16,24},{20,28},{24,32},{28,36},{32,40... | collective-permute-start | bytes 122888 | tf_op jit(solution)/shard_map/ppermute | solution.py:262
  21.2 10.5 %collective-permute-start.3 = (f32[8,128]{1,0:T(8,128)S(1)}, f32[8,128]{1,0:T(8,128)S(1)}, u32[]{:S(2)}, u32[]{:S(2)}) collective-permute-start(f32[8,128]{1,0:T(8,128)S(1)} %pad_maximum_fusion.4), channel_id=1, source_target_pairs={{8,0},{12,4},{16,8},{20,12},{24,16},{28,20},{32,24},{36,28},{40,32... | collective-permute-start | bytes 12296 | tf_op jit(solution)/shard_map/ppermute | solution.py:262
  31.8 0.3 collective-permute-done
  32.1 1.0 %collective-permute-done.3 = f32[8,128]{1,0:T(8,128)S(1)} collective-permute-done((f32[8,128]{1,0:T(8,128)S(1)}, f32[8,128]{1,0:T(8,128)S(1)}, u32[]{:S(2)}, u32[]{:S(2)}) %collective-permute-start.3) | collective-permute-done | bytes 4128 | tf_op jit(solution)/shard_map/ppermute | solution.py:262
  33.1 0.0 collective-permute-done.2
  33.1 0.0 collective-permute-done.1
  33.2 0.1 fusion.1
  33.3 0.1 reshape.63
  33.4 0.3 concatenate.42
  33.7 1.9 %collective-permute-start.5 = (f32[318,128]{1,0:T(8,128)S(1)}, f32[318,128]{1,0:T(8,128)S(1)}, u32[]{:S(2)}, u32[]{:S(2)}) collective-permute-start(f32[318,128]{1,0:T(8,128)S(1)} %concatenate.42), channel_id=1, source_target_pairs={{1,0},{2,1},{3,2},{5,4},{6,5},{7,6},{9,8},{10,9},{11,10},{13,12},{... | collective-permute-start | bytes 488456 | tf_op jit(solution)/shard_map/ppermute | solution.py:262
  35.6 0.1 reshape.61
  35.7 0.3 concatenate.41
  36.0 2.4 %collective-permute-start.4 = (f32[318,128]{1,0:T(8,128)S(1)}, f32[318,128]{1,0:T(8,128)S(1)}, u32[]{:S(2)}, u32[]{:S(2)}) collective-permute-start(f32[318,128]{1,0:T(8,128)S(1)} %concatenate.41), channel_id=1, source_target_pairs={{0,1},{1,2},{2,3},{4,5},{5,6},{6,7},{8,9},{9,10},{10,11},{12,13},{... | collective-permute-start | bytes 488456 | tf_op jit(solution)/shard_map/ppermute | solution.py:262
  38.4 0.1 pad.11.clone
  38.5 0.1 pad_add_fusion.meta
  38.6 0.1 concatenate.44
  38.7 0.0 collective-permute-done.5
  38.7 0.1 reshape.64
  38.8 3.9 %collective-permute-done.4 = f32[318,128]{1,0:T(8,128)S(1)} collective-permute-done((f32[318,128]{1,0:T(8,128)S(1)}, f32[318,128]{1,0:T(8,128)S(1)}, u32[]{:S(2)}, u32[]{:S(2)}) %collective-permute-start.4) | collective-permute-done | bytes 162848 | tf_op jit(solution)/shard_map/ppermute | solution.py:262
  42.7 0.1 reshape.62
  42.8 0.2 maximum_maximum_fusion.c_ref
  43.0 14.6 %shard_map.55 = f32[5,5,4,8,64]{4,3,2,1,0:T(8,128)S(1)} custom-call(s32[2]{0:T(128)S(1)} %pad_add_fusion.meta, f32[14,7,16,128]{3,2,1,0:T(8,128)S(1)} %maximum_maximum_fusion.c_ref, f32[3,6,512]{2,1,0:T(8,128)S(1)} %pad_maximum_fusion.2.f_ref), custom_call_target="tpu_custom_call" | custom-call | tf_op jit(solution)/shard_map/pallas_call | solution.py:302
  57.6 0.1 copy.6
  57.7 0.9 %reshape.66 = f32[125,1,256]{2,1,0:T(1,128)} reshape(f32[5,5,5,4,64]{4,3,2,1,0:T(4,128)S(1)} %copy.6) | data formatting | bytes 256000 | tf_op jit(solution)/shard_map/reshape | solution.py:322
  (26 shorter events, 0.2 us)
Async XLA Ops:
  2.3 0.7 %copy-start.1 = (f32[1,1,512]{2,1,0:T(1,128)S(1)}, f32[1,1,512]{2,1,0:T(1,128)}, u32[]{:S(2)}) copy-start(f32[1,1,512]{2,1,0:T(1,128)} %param.9) | copy-start | bytes 6148
  2.4 0.7 %copy-start = (f32[2,1024]{1,0:T(2,128)S(1)}, f32[2,1024]{1,0:T(2,128)}, u32[]{:S(2)}) copy-start(f32[2,1024]{1,0:T(2,128)} %param.6) | copy-start | bytes 24580
  3.1 30.0 %collective-permute-start.2 = (f32[232,128]{1,0:T(8,128)S(1)}, f32[232,128]{1,0:T(8,128)S(1)}, u32[]{:S(2)}, u32[]{:S(2)}) collective-permute-start(f32[232,128]{1,0:T(8,128)S(1)} %pad_maximum_fusion.1), channel_id=1, source_target_pairs={{4,0},{8,4},{12,8},{16,12},{20,16},{24,20},{28,24},{32,28},{36,32}... | collective-permute-start | bytes 356360 | tf_op jit(solution)/shard_map/ppermute | solution.py:262
  17.3 15.8 %collective-permute-start.1 = (f32[232,128]{1,0:T(8,128)S(1)}, f32[232,128]{1,0:T(8,128)S(1)}, u32[]{:S(2)}, u32[]{:S(2)}) collective-permute-start(f32[232,128]{1,0:T(8,128)S(1)} %pad_maximum_fusion.1), channel_id=1, source_target_pairs={{0,4},{4,8},{8,12},{12,16},{16,20},{20,24},{24,28},{28,32},{32,36}... | collective-permute-start | bytes 356360 | tf_op jit(solution)/shard_map/ppermute | solution.py:262
  19.3 12.8 %collective-permute-start = (f32[80,128]{1,0:T(8,128)S(1)}, f32[80,128]{1,0:T(8,128)S(1)}, u32[]{:S(2)}, u32[]{:S(2)}) collective-permute-start(f32[80,128]{1,0:T(8,128)S(1)} %pad_maximum_fusion.3), channel_id=1, source_target_pairs={{0,8},{4,12},{8,16},{12,20},{16,24},{20,28},{24,32},{28,36},{32,40... | collective-permute-start | bytes 122888 | tf_op jit(solution)/shard_map/ppermute | solution.py:262
  21.2 11.9 %collective-permute-start.3 = (f32[8,128]{1,0:T(8,128)S(1)}, f32[8,128]{1,0:T(8,128)S(1)}, u32[]{:S(2)}, u32[]{:S(2)}) collective-permute-start(f32[8,128]{1,0:T(8,128)S(1)} %pad_maximum_fusion.4), channel_id=1, source_target_pairs={{8,0},{12,4},{16,8},{20,12},{24,16},{28,20},{32,24},{36,28},{40,32... | collective-permute-start | bytes 12296 | tf_op jit(solution)/shard_map/ppermute | solution.py:262
  33.7 5.0 %collective-permute-start.5 = (f32[318,128]{1,0:T(8,128)S(1)}, f32[318,128]{1,0:T(8,128)S(1)}, u32[]{:S(2)}, u32[]{:S(2)}) collective-permute-start(f32[318,128]{1,0:T(8,128)S(1)} %concatenate.42), channel_id=1, source_target_pairs={{1,0},{2,1},{3,2},{5,4},{6,5},{7,6},{9,8},{10,9},{11,10},{13,12},{... | collective-permute-start | bytes 488456 | tf_op jit(solution)/shard_map/ppermute | solution.py:262
  36.0 6.6 %collective-permute-start.4 = (f32[318,128]{1,0:T(8,128)S(1)}, f32[318,128]{1,0:T(8,128)S(1)}, u32[]{:S(2)}, u32[]{:S(2)}) collective-permute-start(f32[318,128]{1,0:T(8,128)S(1)} %concatenate.41), channel_id=1, source_target_pairs={{0,1},{1,2},{2,3},{4,5},{5,6},{6,7},{8,9},{9,10},{10,11},{12,13},{... | collective-permute-start | bytes 488456 | tf_op jit(solution)/shard_map/ppermute | solution.py:262

commit v2 on v1

--- a/solution.py
+++ b/solution.py
@@ -29,13 +29,14 @@
     return (dx + 1) * 9 + (dy + 1) * 3 + dz + 1
 
 
-def body(meta, c_ref, f_ref, out_ref, kf, inv_ref, fd, pat, bands, fp, gs, s3, ap, b3, acc_ref):
-    gx = meta[0]
-    gy = meta[1]
+def body(c_ref, f_ref, out_ref, kf, inv_ref, fd, pat, bands, fp, gs, s3, ap, b3, acc_ref):
+    gx = lax.axis_index("gx")
+    gy = lax.axis_index("gy")
     odd_dev = lax.rem(gx, 2)
     zl = lax.broadcasted_iota(jnp.int32, (16, 128), 1)
     yi = lax.broadcasted_iota(jnp.int32, (16, 128), 0)
     yg = gy * 8 + yi - 3
+    y_in = (yg >= 0) & (yg < 32)
     y_odd = lax.rem(yi, 2) == 0
 
     e8 = lax.broadcasted_iota(jnp.int32, (8, 128), 0)
@@ -46,13 +47,13 @@
 
     wsum = [jnp.zeros((16, 128), F32) for _ in range(6)]
     for o, (dx, dy, dz) in enumerate(FORWARD):
-        ok = (yg + dy >= 0) & (yg + dy < 32) & (zl + dz >= 0) & (zl + dz < 128)
+        ok = y_in & (yg + dy >= 0) & (yg + dy < 32) & (zl + dz >= 0) & (zl + dz < 128)
         for x in range(-3, 4):
             if dx == 0 and x == -3:
                 continue
-            m = jnp.where(ok, c_ref[o, x + 3], F32(0.0))
-            if dx:
-                m = m * (2 * gx + x + 1 < 256).astype(F32)
+            xg = jnp.full((16, 128), 2 * gx + x, jnp.int32)
+            x_ok = (xg >= 0) & (xg + dx < 256)
+            m = jnp.where(ok & x_ok, c_ref[o, x + 3], F32(0.0))
             if x >= -2:
                 kf[kid(dx, dy, dz), x + 2] = -m
                 wsum[x + 2] = wsum[x + 2] + m
@@ -69,13 +70,26 @@
     x_own = 1 - odd_dev
     x_par = 2 - 3 * odd_dev
     x_oth = 5 * odd_dev - 2
-    sides = ((0, 1, 2), (1, 0, 2), (3, 4, 5))
+    s_par = 3 - 2 * odd_dev
+    s_oth = 1 + 2 * odd_dev
+    s_far = 4 * odd_dev
+    sides = ((2, s_par, 2), (s_par, 2, 2), (s_oth, s_far, s_oth))
+
+    def slot_row(dev, place, first):
+        rows = [f_ref[dev, place, first + i : first + i + 1, :] for i in range(4)]
+        return jnp.concatenate(rows, axis=1)
+
     d24 = lax.broadcasted_iota(jnp.int32, (24, 512), 0) - 8
     for dev, (ylo, ny, yout) in enumerate(((6, 2, 0), (0, 8, 2), (0, 2, 10))):
         for side, (own, par, tr) in enumerate(sides):
-            co = f_ref[dev, own : own + 1].astype(jnp.int32) & 1023
-            cp = f_ref[dev, par : par + 1].astype(jnp.int32) & 1023
-            t = f_ref[dev, tr : tr + 1]
+            co = slot_row(dev, own, 0).astype(jnp.int32) & 1023
+            cp = slot_row(dev, par, 0).astype(jnp.int32) & 1023
+            reach = (gy + dev >= 1) & (gy + dev < 5)
+            if side == 2:
+                mate = gx + 4 * odd_dev - 2
+                reach = reach & (mate >= 0) & (mate < 128)
+            known = jnp.full((1, 512), reach.astype(jnp.int32), jnp.int32) > 0
+            t = jnp.where(known, slot_row(dev, tr, 4), F32(0.0))
             delta = (cp & 127) - (co & 127)
             bt = jnp.where(d24 == delta, t, F32(0.0))
             hi = bt.astype(jnp.bfloat16)
@@ -102,7 +116,9 @@
 
     for x in range(-2, 4):
         diag = c_ref[13, x + 3] + wsum[x + 2] + fd[x + 2]
-        inv = jnp.where(diag > 0.0, 1.0 / diag, F32(0.0))
+        xg = jnp.full((16, 128), 2 * gx + x, jnp.int32)
+        inv = jnp.where(y_in & (xg >= 0) & (xg < 256), 1.0 / diag, F32(0.0))
+        diag = jnp.where(y_in & (xg >= 0) & (xg < 256), diag, F32(0.0))
         kf[13, x + 2] = diag
         inv_ref[x + 2] = inv
         for dz in (-1, 0, 1):
@@ -244,65 +260,168 @@
     lax.fori_loop(0, 4, restrict, 0)
 
 
-def per_device(trans, storage, fault_cells, fault_count, fault_trans):
+SOURCES = (
+    (-2, 0, 1, 1, 4, 9),
+    (-1, 1, 2, 0, 0, 14),
+    (0, 3, 2, 0, 0, 14),
+    (1, 5, 2, 0, 0, 14),
+    (2, None, 0, 0, 0, 0),
+)
+
+
+def exchange(core, fault, wide, slots, send, recv, ysend, yrecv, local):
     gx = lax.axis_index("gx")
     gy = lax.axis_index("gy")
-    n_gx = lax.axis_size("gx")
-    n_gy = lax.axis_size("gy")
+
+    def has(i):
+        return (gx + i >= 0) & (gx + i < 128)
+
+    def has_y(j):
+        return (gy + j >= 0) & (gy + j < 4)
+
+    barrier = pltpu.get_barrier_semaphore()
+    count = 0
+    for i in (-2, -1, 1, 2):
+        count = count + has(i).astype(jnp.int32)
+
+        @pl.when(has(i))
+        def _(i=i):
+            pl.semaphore_signal(
+                barrier, inc=1, device_id=(gx + i, gy), device_id_type=pl.DeviceIdType.MESH
+            )
+
+    for j in (-1, 1):
+        count = count + has_y(j).astype(jnp.int32)
+
+        @pl.when(has_y(j))
+        def _(j=j):
+            pl.semaphore_signal(
+                barrier, inc=1, device_id=(gx, gy + j), device_id_type=pl.DeviceIdType.MESH
+            )
+
+    keep = pltpu.make_async_copy(core, wide.at[:, 3:5, 3:11], local.at[0])
+    keep.start()
+    keep_fault = pltpu.make_async_copy(fault, slots.at[1, 2], local.at[1])
+    keep_fault.start()
+    pl.semaphore_wait(barrier, count)
+
+    def along_x(n):
+        i, x0, nx, own, o0, no = SOURCES[n]
+        to = (gx - i, gy)
+        copies = []
+        if no:
+            copies.append(
+                pltpu.make_async_remote_copy(
+                    core.at[o0 : o0 + no, own : own + nx],
+                    wide.at[o0 : o0 + no, x0 : x0 + nx, 3:11],
+                    send.at[n, 0],
+                    recv.at[n, 0],
+                    device_id=to,
+                    device_id_type=pl.DeviceIdType.MESH,
+                )
+            )
+        copies.append(
+            pltpu.make_async_remote_copy(
+                fault,
+                slots.at[1, n],
+                send.at[n, 1],
+                recv.at[n, 1],
+                device_id=to,
+                device_id_type=pl.DeviceIdType.MESH,
+            )
+        )
+        return copies
+
+    def along_y(n, j):
+        i, x0, nx, own, o0, no = SOURCES[n]
+        to = (gx, gy + j)
+        s = (j + 1) // 2
+        y0, y1 = (8, 0) if j == 1 else (3, 11)
+        place = 0 if j == 1 else 2
+        copies = []
+        if no:
+            if n == 2:
+                source = core.at[:, :, y0 - 3 : y0]
+            else:
+                source = wide.at[o0 : o0 + no, x0 : x0 + nx, y0 : y0 + 3]
+            copies.append(
+                pltpu.make_async_remote_copy(
+                    source,
+                    wide.at[o0 : o0 + no, x0 : x0 + nx, y1 : y1 + 3],
+                    ysend.at[s, n, 0],
+                    yrecv.at[s, n, 0],
+                    device_id=to,
+                    device_id_type=pl.DeviceIdType.MESH,
+                )
+            )
+        copies.append(
+            pltpu.make_async_remote_copy(
+                fault if n == 2 else slots.at[1, n],
+                slots.at[place, n],
+                ysend.at[s, n, 1],
+                yrecv.at[s, n, 1],
+                device_id=to,
+                device_id_type=pl.DeviceIdType.MESH,
+            )
+        )
+        return copies
+
+    def guarded(ok, copies, what):
+        @pl.when(ok)
+        def _():
+            for c in copies:
+                getattr(c, what)()
+
+    for n in (0, 1, 3, 4):
+        guarded(has(-SOURCES[n][0]), along_x(n), "start")
+    for j in (-1, 1):
+        guarded(has_y(j), along_y(2, j), "start")
+    for n in (1, 3, 4, 0):
+        guarded(has(SOURCES[n][0]), along_x(n), "wait_recv")
+        for j in (-1, 1):
+            guarded(has(SOURCES[n][0]) & has_y(j), along_y(n, j), "start")
+    for n in (0, 1, 3, 4):
+        guarded(has(-SOURCES[n][0]), along_x(n), "wait_send")
+    for n in range(5):
+        for j in (-1, 1):
+            guarded(has(SOURCES[n][0]) & has_y(j), along_y(n, j), "wait_send")
+            guarded(has(SOURCES[n][0]) & has_y(-j), along_y(n, j), "wait_recv")
+    keep.wait()
+    keep_fault.wait()
+
+
+def per_device(trans, storage, fault_cells, fault_count, fault_trans):
     slots = jnp.arange(512, dtype=jnp.int32)
     live = jnp.where(slots < fault_count.reshape(()), fault_trans.reshape(-1), F32(0.0))
     cells = fault_cells.reshape(-1).astype(F32)
     fault = jnp.concatenate([cells.reshape(4, 128), live.reshape(4, 128)], axis=0)
     core = jnp.concatenate(
-        [trans.reshape(13, 2, 8, 128), storage.reshape(1, 2, 8, 128)], axis=0
+        [trans.reshape(13, 2, 8, 1, 128), storage.reshape(1, 2, 8, 1, 128)], axis=0
     )
-
-    def shift(value, axis, size, by):
-        pairs = [(i, i + by) for i in range(size) if 0 <= i + by < size]
-        return lax.ppermute(value, axis, pairs)
-
-    packed = jnp.concatenate([core.reshape(224, 128), fault], axis=0)
-    left = shift(packed, "gx", n_gx, 1)
-    right = shift(packed, "gx", n_gx, -1)
-    second = jnp.concatenate([core[4:13, 1].reshape(72, 128), fault], axis=0)
-    left2 = shift(second, "gx", n_gx, 2)
-    right2 = shift(fault, "gx", n_gx, -2)
-    far = jnp.concatenate(
-        [
-            jnp.zeros((4, 1, 8, 128), F32),
-            left2[:72].reshape(9, 1, 8, 128),
-            jnp.zeros((1, 1, 8, 128), F32),
+    vm = pl.BlockSpec(memory_space=pltpu.VMEM)
+    hbm = pl.BlockSpec(memory_space=pl.ANY)
+    wide, faults = pl.pallas_call(
+        exchange,
+        out_shape=(
+            jax.ShapeDtypeStruct((14, 7, 16, 1, 128), F32),
+            jax.ShapeDtypeStruct((3, 5, 8, 128), F32),
+        ),
+        in_specs=[vm, vm],
+        out_specs=(hbm, hbm),
+        scratch_shapes=[
+            pltpu.SemaphoreType.DMA((5, 2)),
+            pltpu.SemaphoreType.DMA((5, 2)),
+            pltpu.SemaphoreType.DMA((2, 5, 2)),
+            pltpu.SemaphoreType.DMA((2, 5, 2)),
+            pltpu.SemaphoreType.DMA((2,)),
         ],
-        axis=0,
-    )
-    wide = jnp.concatenate(
-        [far, left[:224].reshape(14, 2, 8, 128), core, right[:224].reshape(14, 2, 8, 128)], axis=1
-    )
-    even = lax.rem(gx, 2) == 0
-    partner = jnp.where(even, right[224:228], left[224:228])
-    other = jnp.where(even, left[224:], right[224:])
-    beyond = jnp.where(even, left2[72:76], right2[:4])
-    faults = jnp.concatenate([fault[:4], partner, fault[4:], other[:4], beyond, other[4:]], axis=0)
-    up = jnp.concatenate([wide[:, :, 5:].reshape(294, 128), faults], axis=0)
-    down = jnp.concatenate([wide[:, :, :3].reshape(294, 128), faults], axis=0)
-    below = shift(up, "gy", n_gy, 1)
-    above = shift(down, "gy", n_gy, -1)
-    full = jnp.concatenate(
-        [
-            below[:294].reshape(14, 7, 3, 128),
-            wide,
-            above[:294].reshape(14, 7, 3, 128),
-            jnp.zeros((14, 7, 2, 128), F32),
-        ],
-        axis=2,
-    )
-    slots3 = jnp.stack([below[294:], faults, above[294:]]).reshape(3, 6, 512)
-    meta = jnp.stack([gx, gy]).astype(jnp.int32)
-    vm = pl.BlockSpec(memory_space=pltpu.VMEM)
+        compiler_params=pltpu.CompilerParams(collective_id=0, has_side_effects=True),
+    )(core, fault)
+    full = wide.reshape(14, 7, 16, 128)
     out = pl.pallas_call(
         body,
         out_shape=jax.ShapeDtypeStruct((5, 5, 4, 8, 64), F32),
-        in_specs=[pl.BlockSpec(memory_space=pltpu.SMEM), vm, vm],
+        in_specs=[vm, vm],
         out_specs=vm,
         scratch_shapes=[
             pltpu.VMEM((27, 6, 16, 128), F32),
@@ -318,7 +437,7 @@
             pltpu.VMEM((5, 5, 8, 128), F32),
         ],
         compiler_params=pltpu.CompilerParams(vmem_limit_bytes=48 * 1024 * 1024),
-    )(meta, full, slots3)
+    )(full, faults)
     return out[:, :, :, :5].transpose(0, 1, 3, 2, 4).reshape(125, 1, 256)
 
 

time: 58.9 us -> 46.7 us (0.79)
  the two profiles are of different devices: /device:TPU:24 before, /device:TPU:17 now
where the time goes in v2:
time: 46.7 us; the launch traced here: 46.4 us
  Pallas kernels  38.8 us (83%)
  local copies, waits for them, and re-layouts  5.48 us (12%)
  other arithmetic  1.36 us (3%)
  between operations  0.71 us (2%)
    pallas_call x1, Pallas kernels, per_device(): pl.pallas_call(exchange, out_shape=(jax.ShapeDtypeStruct((14, 7, 16, 1, 1...  25.2 us
    pallas_call x1, Pallas kernels, per_device(): pl.pallas_call(body, out_shape=jax.ShapeDtypeStruct((5, 5, 4, 8, 64), F32...  13.7 us
    unnamed x10, local copies, waits for them, and re-layouts  3.41 us
    reshape x1, local copies, waits for them, and re-layouts, per_device(): trans.reshape(13, 2, 8, 1, 128)  1.06 us

profile of v2, /device:TPU:17, one launch (start us, length us, event | category | flops | bytes accessed | tf_op | source)
XLA Modules:
  0.0 46.4 jit_solution(3201214476322881143)
XLA Ops:
  0.7 0.0 copy-start.3
  0.7 0.7 %copy-done.3 = f32[1,1,512]{2,1,0:T(1,128)S(1)} copy-done((f32[1,1,512]{2,1,0:T(1,128)S(1)}, f32[1,1,512]{2,1,0:T(1,128)}, u32[]{:S(2)}) %copy-start.3) | copy-done | bytes 2072
  1.3 0.0 copy-start.4
  1.3 0.7 %copy-done.4 = s32[1,1,512]{2,1,0:T(1,128)S(1)} copy-done((s32[1,1,512]{2,1,0:T(1,128)S(1)}, s32[1,1,512]{2,1,0:T(1,128)}, u32[]{:S(2)}) %copy-start.4) | copy-done | bytes 2072
  2.0 0.0 copy-start.2
  2.0 0.6 %pad_maximum_fusion.1.fault = f32[8,128]{1,0:T(8,128)} fusion(f32[4,128]{1,0:T(4,128)S(1)} %fusion, f32[4,128]{1,0:T(4,128)S(1)} %bitcast.8), kind=kLoop, calls=%fused_computation.2 | loop fusion | flops 1024 | bytes 8192 | tf_op jit(solution)/shard_map/concatenate | solution.py:397
  2.6 0.1 copy-done.2
  2.7 1.1 %reshape.25 = f32[13,2,8,1,128]{4,3,2,1,0:T(1,128)S(1)} reshape(f32[13,2,1024]{2,1,0:T(2,128)} %param.5) | data formatting | bytes 212992 | tf_op jit(solution)/shard_map/reshape | solution.py:399
  3.8 0.8 %pad_maximum_fusion.core = f32[14,2,8,1,128]{4,3,2,1,0:T(1,128)} fusion(f32[1,2,8,1,128]{4,3,2,1,0:T(1,128)S(1)} %reshape.26, f32[13,2,8,1,128]{4,3,2,1,0:T(1,128)S(1)} %reshape.25), kind=kLoop, calls=%fused_computation.1 | loop fusion | flops 28672 | bytes 229376 | tf_op jit(solution)/shard_map/concatenate | solution.py:398
  4.6 25.2 %shard_map.55 = (f32[14,7,16,1,128]{4,3,2,1,0:T(1,128)}, f32[3,5,8,128]{3,2,1,0:T(8,128)}) custom-call(f32[14,2,8,1,128]{4,3,2,1,0:T(1,128)} %pad_maximum_fusion.core, f32[8,128]{1,0:T(8,128)} %pad_maximum_fusion.1.fault), custom_call_target="tpu_custom_call" | custom-call | tf_op jit(solution)/shard_map/pallas_call | solution.py:403
  29.7 0.0 copy-start
  29.8 1.1 %copy-done = f32[14,7,16,1,128]{4,3,2,1,0:T(1,128)S(1)} copy-done((f32[14,7,16,1,128]{4,3,2,1,0:T(1,128)S(1)}, f32[14,7,16,1,128]{4,3,2,1,0:T(1,128)}, u32[]{:S(2)}) %copy-start) | copy-done | bytes 802840
  30.9 0.0 copy-start.1
  30.9 0.8 %copy-done.1 = f32[3,5,8,128]{3,2,1,0:T(8,128)S(1)} copy-done((f32[3,5,8,128]{3,2,1,0:T(8,128)S(1)}, f32[3,5,8,128]{3,2,1,0:T(8,128)}, u32[]{:S(2)}) %copy-start.1) | copy-done | bytes 61464
  31.7 13.7 %shard_map.56 = f32[5,5,4,8,64]{4,3,2,1,0:T(8,128)S(1)} custom-call(f32[14,7,16,128]{3,2,1,0:T(8,128)S(1)} %bitcast.7, f32[3,5,8,128]{3,2,1,0:T(8,128)S(1)} %copy-done.1), custom_call_target="tpu_custom_call" | custom-call | tf_op jit(solution)/shard_map/pallas_call | solution.py:421
  45.4 0.1 copy.6
  45.5 0.9 %reshape.31 = f32[125,1,256]{2,1,0:T(1,128)} reshape(f32[5,5,5,4,64]{4,3,2,1,0:T(4,128)S(1)} %copy.6) | data formatting | bytes 256000 | tf_op jit(solution)/shard_map/reshape | solution.py:441
  (4 shorter events, 0.1 us)
Async XLA Ops:
  0.7 0.7 %copy-start.3 = (f32[1,1,512]{2,1,0:T(1,128)S(1)}, f32[1,1,512]{2,1,0:T(1,128)}, u32[]{:S(2)}) copy-start(f32[1,1,512]{2,1,0:T(1,128)} %param.9) | copy-start | bytes 6148
  1.3 0.7 %copy-start.4 = (s32[1,1,512]{2,1,0:T(1,128)S(1)}, s32[1,1,512]{2,1,0:T(1,128)}, u32[]{:S(2)}) copy-start(s32[1,1,512]{2,1,0:T(1,128)} %param.7) | copy-start | bytes 6148
  2.0 0.7 %copy-start.2 = (f32[2,1024]{1,0:T(2,128)S(1)}, f32[2,1024]{1,0:T(2,128)}, u32[]{:S(2)}) copy-start(f32[2,1024]{1,0:T(2,128)} %param.6) | copy-start | bytes 24580
  29.7 1.1 %copy-start = (f32[14,7,16,1,128]{4,3,2,1,0:T(1,128)S(1)}, f32[14,7,16,1,128]{4,3,2,1,0:T(1,128)}, u32[]{:S(2)}) copy-start(f32[14,7,16,1,128]{4,3,2,1,0:T(1,128)} %get-tuple-element.7) | copy-start | bytes 2408452
  30.9 0.8 %copy-start.1 = (f32[3,5,8,128]{3,2,1,0:T(8,128)S(1)}, f32[3,5,8,128]{3,2,1,0:T(8,128)}, u32[]{:S(2)}) copy-start(f32[3,5,8,128]{3,2,1,0:T(8,128)} %get-tuple-element.8.f_ref) | copy-start | bytes 184324

commit v3 on v2

--- a/solution.py
+++ b/solution.py
@@ -29,7 +29,13 @@
     return (dx + 1) * 9 + (dy + 1) * 3 + dz + 1
 
 
-def body(c_ref, f_ref, out_ref, kf, inv_ref, fd, pat, bands, fp, gs, s3, ap, b3, acc_ref):
+def body(n_any, c_any, fc_any, ft_any, out_ref, counts, c_ref, fc_ref, ft_ref, sems, kf, inv_ref, fd, pat, bands, fp, gs, s3, ap, b3, acc_ref, cols):
+    loads = []
+    for n, (a, b) in enumerate(
+        ((n_any, counts), (fc_any, fc_ref), (ft_any, ft_ref), (c_any, c_ref))
+    ):
+        loads.append(pltpu.make_async_copy(a, b, sems.at[n]))
+        loads[n].start()
     gx = lax.axis_index("gx")
     gy = lax.axis_index("gy")
     odd_dev = lax.rem(gx, 2)
@@ -44,6 +50,9 @@
     for d in range(17):
         col = lax.rem(lax.shift_right_logical(z8 + (d - 8 + 160), 1), 5)
         pat[d] = jnp.where(col == e8, F32(1.0), F32(0.0))
+
+    for load in loads:
+        load.wait()
 
     wsum = [jnp.zeros((16, 128), F32) for _ in range(6)]
     for o, (dx, dy, dz) in enumerate(FORWARD):
@@ -75,35 +84,40 @@
     s_far = 4 * odd_dev
     sides = ((2, s_par, 2), (s_par, 2, 2), (s_oth, s_far, s_oth))
 
-    def slot_row(dev, place, first):
-        rows = [f_ref[dev, place, first + i : first + i + 1, :] for i in range(4)]
-        return jnp.concatenate(rows, axis=1)
-
-    d24 = lax.broadcasted_iota(jnp.int32, (24, 512), 0) - 8
+    def slot_row(ref, dev, place):
+        return jnp.concatenate([ref[dev, place, i] for i in range(4)], axis=1)
+
+    zrow = lax.broadcasted_iota(jnp.int32, (128, 512), 0)
+    slot = lax.broadcasted_iota(jnp.int32, (1, 512), 1)
     for dev, (ylo, ny, yout) in enumerate(((6, 2, 0), (0, 8, 2), (0, 2, 10))):
         for side, (own, par, tr) in enumerate(sides):
-            co = slot_row(dev, own, 0).astype(jnp.int32) & 1023
-            cp = slot_row(dev, par, 0).astype(jnp.int32) & 1023
+            co = slot_row(fc_ref, dev, own) & 1023
+            cp = slot_row(fc_ref, dev, par) & 1023
             reach = (gy + dev >= 1) & (gy + dev < 5)
             if side == 2:
                 mate = gx + 4 * odd_dev - 2
                 reach = reach & (mate >= 0) & (mate < 128)
-            known = jnp.full((1, 512), reach.astype(jnp.int32), jnp.int32) > 0
-            t = jnp.where(known, slot_row(dev, tr, 4), F32(0.0))
-            delta = (cp & 127) - (co & 127)
-            bt = jnp.where(d24 == delta, t, F32(0.0))
-            hi = bt.astype(jnp.bfloat16)
-            r1 = bt - hi.astype(F32)
-            mid = r1.astype(jnp.bfloat16)
-            low = (r1 - mid.astype(F32)).astype(jnp.bfloat16)
-            rows = lax.broadcasted_iota(jnp.int32, (ny * 128, 512), 0) + ylo * 128
-            hot = jnp.where(rows == co, F32(1.0), F32(0.0)).astype(jnp.bfloat16)
-            dims = (((1,), (1,)), ((), ()))
-            got = lax.dot_general(hi, hot, dims, preferred_element_type=F32)
-            got = got + lax.dot_general(mid, hot, dims, preferred_element_type=F32)
-            got = got + lax.dot_general(low, hot, dims, preferred_element_type=F32)
-            for y in range(ny):
-                bands[side, yout + y] = got[:, y * 128 : (y + 1) * 128]
+            count = jnp.concatenate([counts[dev, tr]] * 4, axis=1)
+            alive = jnp.where(jnp.full((1, 512), reach.astype(jnp.int32)) > 0, count, 0)
+            t = jnp.where(slot < alive, slot_row(ft_ref, dev, tr), F32(0.0))
+            zo = co & 127
+            key = (lax.shift_right_logical(co, 7) - ylo) * 24 + (cp & 127) - zo + 8
+            hit = lax.broadcasted_iota(jnp.int32, (ny * 24, 512), 0) == key
+            hi = t.astype(jnp.bfloat16).astype(F32)
+            mid = (t - hi).astype(jnp.bfloat16).astype(F32)
+            parts = [
+                jnp.where(hit, p, F32(0.0)).astype(jnp.bfloat16) for p in (hi, mid, t - hi - mid)
+            ]
+            hot = jnp.where(zrow == zo, F32(1.0), F32(0.0)).astype(jnp.bfloat16)
+            got = lax.dot_general(
+                jnp.concatenate(parts, axis=0),
+                hot,
+                (((1,), (1,)), ((), ())),
+                preferred_element_type=F32,
+            )
+            n = ny * 24
+            got = got[:n] + got[n : 2 * n] + got[2 * n :]
+            bands[side, yout : yout + ny] = got.reshape(ny, 24, 128)
 
     fd[...] = jnp.zeros((6, 16, 128), F32)
     for side, xs in enumerate((x_own, x_par, x_oth)):
@@ -254,10 +268,15 @@
             for ry in range(5):
                 b = lax.rem(gy * 4 + yc + ry + 3, 5)
                 q = (rx * 5 + ry) * 8
-                out_ref[a, b, yc] = got[q : q + 8]
+                cols[a, b, yc] = got[q : q + 8]
         return carry
 
     lax.fori_loop(0, 4, restrict, 0)
+    for a in range(5):
+        for b in range(5):
+            tile = jnp.concatenate([cols[a, b, yc] for yc in range(4)], axis=1)
+            c = (a * 5 + b) * 5
+            out_ref[c : c + 5, 0, :] = tile[:5]
 
 
 SOURCES = (
@@ -269,7 +288,7 @@
 )
 
 
-def exchange(core, fault, wide, slots, send, recv, ysend, yrecv, local):
+def exchange(trans, storage, cells, weights, count, wide, slot_c, slot_t, slot_n, send, recv, ysend, yrecv, local):
     gx = lax.axis_index("gx")
     gy = lax.axis_index("gy")
 
@@ -280,9 +299,9 @@
         return (gy + j >= 0) & (gy + j < 4)
 
     barrier = pltpu.get_barrier_semaphore()
-    count = 0
+    count_in = 0
     for i in (-2, -1, 1, 2):
-        count = count + has(i).astype(jnp.int32)
+        count_in = count_in + has(i).astype(jnp.int32)
 
         @pl.when(has(i))
         def _(i=i):
@@ -291,7 +310,7 @@
             )
 
     for j in (-1, 1):
-        count = count + has_y(j).astype(jnp.int32)
+        count_in = count_in + has_y(j).astype(jnp.int32)
 
         @pl.when(has_y(j))
         def _(j=j):
@@ -299,72 +318,62 @@
                 barrier, inc=1, device_id=(gx, gy + j), device_id_type=pl.DeviceIdType.MESH
             )
 
-    keep = pltpu.make_async_copy(core, wide.at[:, 3:5, 3:11], local.at[0])
-    keep.start()
-    keep_fault = pltpu.make_async_copy(fault, slots.at[1, 2], local.at[1])
-    keep_fault.start()
-    pl.semaphore_wait(barrier, count)
-
-    def along_x(n):
-        i, x0, nx, own, o0, no = SOURCES[n]
-        to = (gx - i, gy)
-        copies = []
-        if no:
-            copies.append(
-                pltpu.make_async_remote_copy(
-                    core.at[o0 : o0 + no, own : own + nx],
-                    wide.at[o0 : o0 + no, x0 : x0 + nx, 3:11],
-                    send.at[n, 0],
-                    recv.at[n, 0],
-                    device_id=to,
-                    device_id_type=pl.DeviceIdType.MESH,
-                )
-            )
-        copies.append(
+    def faults(n):
+        return ((cells, slot_c, n), (weights, slot_t, n), (count, slot_n, n))
+
+    keeps = []
+    for x in range(2):
+        keeps.append((trans.at[:, :, x], wide.at[0:13, 3 + x, 3:11]))
+        keeps.append((storage.at[:, x], wide.at[13, 3 + x, 3:11]))
+    for own, slots, n in faults(2):
+        keeps.append((own, slots.at[1, n]))
+    keeps = [pltpu.make_async_copy(a, b, local.at[n]) for n, (a, b) in enumerate(keeps)]
+    for k in keeps:
+        k.start()
+    pl.semaphore_wait(barrier, count_in)
+
+    def remote(pairs, sends, recvs, to):
+        return [
             pltpu.make_async_remote_copy(
-                fault,
-                slots.at[1, n],
-                send.at[n, 1],
-                recv.at[n, 1],
+                a,
+                b,
+                sends.at[k],
+                recvs.at[k],
                 device_id=to,
                 device_id_type=pl.DeviceIdType.MESH,
             )
-        )
-        return copies
+            for k, (a, b) in enumerate(pairs)
+        ]
+
+    def along_x(n):
+        i, x0, nx, own, o0, no = SOURCES[n]
+        pairs = []
+        for x in range(nx):
+            last = min(o0 + no, 13)
+            pairs.append((trans.at[o0:last, :, own + x], wide.at[o0:last, x0 + x, 3:11]))
+            if no == 14:
+                pairs.append((storage.at[:, own + x], wide.at[13, x0 + x, 3:11]))
+        pairs += [(a, slots.at[1, m]) for a, slots, m in faults(n)]
+        return remote(pairs, send.at[n], recv.at[n], (gx - i, gy))
 
     def along_y(n, j):
         i, x0, nx, own, o0, no = SOURCES[n]
-        to = (gx, gy + j)
-        s = (j + 1) // 2
         y0, y1 = (8, 0) if j == 1 else (3, 11)
         place = 0 if j == 1 else 2
-        copies = []
-        if no:
-            if n == 2:
-                source = core.at[:, :, y0 - 3 : y0]
-            else:
-                source = wide.at[o0 : o0 + no, x0 : x0 + nx, y0 : y0 + 3]
-            copies.append(
-                pltpu.make_async_remote_copy(
-                    source,
-                    wide.at[o0 : o0 + no, x0 : x0 + nx, y1 : y1 + 3],
-                    ysend.at[s, n, 0],
-                    yrecv.at[s, n, 0],
-                    device_id=to,
-                    device_id_type=pl.DeviceIdType.MESH,
+        pairs = []
+        if n == 2:
+            for x in range(2):
+                pairs.append(
+                    (trans.at[:, y0 - 3 : y0, x], wide.at[0:13, 3 + x, y1 : y1 + 3])
                 )
-            )
-        copies.append(
-            pltpu.make_async_remote_copy(
-                fault if n == 2 else slots.at[1, n],
-                slots.at[place, n],
-                ysend.at[s, n, 1],
-                yrecv.at[s, n, 1],
-                device_id=to,
-                device_id_type=pl.DeviceIdType.MESH,
-            )
-        )
-        return copies
+                pairs.append((storage.at[y0 - 3 : y0, x], wide.at[13, 3 + x, y1 : y1 + 3]))
+        elif no:
+            cut = wide.at[o0 : o0 + no, x0 : x0 + nx]
+            pairs.append((cut.at[:, :, y0 : y0 + 3], cut.at[:, :, y1 : y1 + 3]))
+        for a, slots, m in faults(n):
+            pairs.append((a if n == 2 else slots.at[1, m], slots.at[place, m]))
+        s = (j + 1) // 2
+        return remote(pairs, ysend.at[s, n], yrecv.at[s, n], (gx, gy + j))
 
     def guarded(ok, copies, what):
         @pl.when(ok)
@@ -386,44 +395,50 @@
         for j in (-1, 1):
             guarded(has(SOURCES[n][0]) & has_y(j), along_y(n, j), "wait_send")
             guarded(has(SOURCES[n][0]) & has_y(-j), along_y(n, j), "wait_recv")
-    keep.wait()
-    keep_fault.wait()
+    for k in keeps:
+        k.wait()
 
 
 def per_device(trans, storage, fault_cells, fault_count, fault_trans):
-    slots = jnp.arange(512, dtype=jnp.int32)
-    live = jnp.where(slots < fault_count.reshape(()), fault_trans.reshape(-1), F32(0.0))
-    cells = fault_cells.reshape(-1).astype(F32)
-    fault = jnp.concatenate([cells.reshape(4, 128), live.reshape(4, 128)], axis=0)
-    core = jnp.concatenate(
-        [trans.reshape(13, 2, 8, 1, 128), storage.reshape(1, 2, 8, 1, 128)], axis=0
-    )
-    vm = pl.BlockSpec(memory_space=pltpu.VMEM)
-    hbm = pl.BlockSpec(memory_space=pl.ANY)
-    wide, faults = pl.pallas_call(
+    any_space = pl.BlockSpec(memory_space=pltpu.HBM)
+    wide, slot_c, slot_t, slot_n = pl.pallas_call(
         exchange,
         out_shape=(
             jax.ShapeDtypeStruct((14, 7, 16, 1, 128), F32),
-            jax.ShapeDtypeStruct((3, 5, 8, 128), F32),
+            jax.ShapeDtypeStruct((3, 5, 4, 1, 128), jnp.int32),
+            jax.ShapeDtypeStruct((3, 5, 4, 1, 128), F32),
+            jax.ShapeDtypeStruct((3, 5, 1, 128), jnp.int32),
         ),
-        in_specs=[vm, vm],
-        out_specs=(hbm, hbm),
+        in_specs=[any_space] * 5,
+        out_specs=(any_space,) * 4,
         scratch_shapes=[
-            pltpu.SemaphoreType.DMA((5, 2)),
-            pltpu.SemaphoreType.DMA((5, 2)),
-            pltpu.SemaphoreType.DMA((2, 5, 2)),
-            pltpu.SemaphoreType.DMA((2, 5, 2)),
-            pltpu.SemaphoreType.DMA((2,)),
+            pltpu.SemaphoreType.DMA((5, 7)),
+            pltpu.SemaphoreType.DMA((5, 7)),
+            pltpu.SemaphoreType.DMA((2, 5, 7)),
+            pltpu.SemaphoreType.DMA((2, 5, 7)),
+            pltpu.SemaphoreType.DMA((7,)),
         ],
-        compiler_params=pltpu.CompilerParams(collective_id=0, has_side_effects=True),
-    )(core, fault)
-    full = wide.reshape(14, 7, 16, 128)
-    out = pl.pallas_call(
+        compiler_params=pltpu.CompilerParams(
+            collective_id=0, has_side_effects=True, vmem_limit_bytes=67043328
+        ),
+    )(
+        trans.reshape(13, 2, 8, 128).transpose(0, 2, 1, 3).reshape(13, 8, 2, 1, 128),
+        storage.reshape(2, 8, 128).transpose(1, 0, 2).reshape(8, 2, 1, 128),
+        fault_cells.reshape(4, 1, 128),
+        fault_trans.reshape(4, 1, 128),
+        jnp.broadcast_to(fault_count.reshape(1, 1), (1, 128)),
+    )
+    return pl.pallas_call(
         body,
-        out_shape=jax.ShapeDtypeStruct((5, 5, 4, 8, 64), F32),
-        in_specs=[vm, vm],
-        out_specs=vm,
+        out_shape=jax.ShapeDtypeStruct((125, 1, 256), F32),
+        in_specs=[any_space] * 4,
+        out_specs=pl.BlockSpec(memory_space=pltpu.VMEM),
         scratch_shapes=[
+            pltpu.VMEM((3, 5, 1, 128), jnp.int32),
+            pltpu.VMEM((14, 7, 16, 128), F32),
+            pltpu.VMEM((3, 5, 4, 1, 128), jnp.int32),
+            pltpu.VMEM((3, 5, 4, 1, 128), F32),
+            pltpu.SemaphoreType.DMA((4,)),
             pltpu.VMEM((27, 6, 16, 128), F32),
             pltpu.VMEM((6, 16, 128), F32),
             pltpu.VMEM((6, 16, 128), F32),
@@ -435,10 +450,10 @@
             pltpu.VMEM((4, 10, 9, 8, 128), F32),
             pltpu.VMEM((3, 4, 10, 9, 8, 128), F32),
             pltpu.VMEM((5, 5, 8, 128), F32),
+            pltpu.VMEM((5, 5, 4, 8, 64), F32),
         ],
-        compiler_params=pltpu.CompilerParams(vmem_limit_bytes=48 * 1024 * 1024),
-    )(full, faults)
-    return out[:, :, :, :5].transpose(0, 1, 3, 2, 4).reshape(125, 1, 256)
+        compiler_params=pltpu.CompilerParams(vmem_limit_bytes=67043328),
+    )(slot_n, wide.reshape(14, 7, 16, 128), slot_c, slot_t)
 
 
 def solution(mesh):

time: 46.7 us -> 40.3 us (0.86)
  local copies, waits for them, and re-layouts: 5.48 us -> 0.58 us
  other arithmetic: 1.36 us -> 0 us
    unnamed x10 -> x0, local copies, waits for them, and re-layouts: 3.41 us -> none
    reshape x3 -> x0, local copies, waits for them, and re-layouts: 1.98 us -> none  [the longest x1 1.06 us: per_device(): trans.reshape(13, 2, 8, 1, 128)]
    concatenate x2 -> x0, other arithmetic: 1.35 us -> none  [the longest x1 0.76 us: per_device(): jnp.concatenate([trans.reshape(13, 2, 8, 1, 128), storage.reshape(1, 2, 8...]
    pallas_call x1, Pallas kernels: 25.2 us -> 26.1 us  [per_device(): pl.pallas_call(exchange, out_shape=(jax.ShapeDtypeStruct((14, 7, 16, 1, 1...]
    pallas_call x1, Pallas kernels: 13.7 us -> 12.7 us  [per_device(): pl.pallas_call(body, out_shape=jax.ShapeDtypeStruct((125, 1, 256), F32),...]
    broadcast_in_dim x0 -> x1, local copies, waits for them, and re-layouts: none -> 0.58 us  [per_device(): jnp.broadcast_to(fault_count.reshape(1, 1), (1, 128))]
where the time goes in v3:
time: 40.3 us; the launch traced here: 40.1 us
  Pallas kernels  38.9 us (97%)
  between operations  0.66 us (2%)
  local copies, waits for them, and re-layouts  0.58 us (1%)
    pallas_call x1, Pallas kernels, per_device(): pl.pallas_call(exchange, out_shape=(jax.ShapeDtypeStruct((14, 7, 16, 1, 1...  26.1 us
    pallas_call x1, Pallas kernels, per_device(): pl.pallas_call(body, out_shape=jax.ShapeDtypeStruct((125, 1, 256), F32),...  12.7 us

profile of v3, /device:TPU:17, one launch (start us, length us, event | category | flops | bytes accessed | tf_op | source)
XLA Modules:
  0.0 40.1 jit_solution(10107195928400266152)
XLA Ops:
  0.7 0.6 %broadcast_in_dim.8.count = s32[1,128]{1,0:T(1,128)} broadcast(s32[]{:T(128)} %bitcast.14), dimensions={} | broadcast | bytes 516 | tf_op jit(solution)/shard_map/broadcast_in_dim | solution.py:429
  1.2 26.1 %shard_map.55 = (f32[14,7,16,1,128]{4,3,2,1,0:T(1,128)}, s32[3,5,4,1,128]{4,3,2,1,0:T(1,128)}, f32[3,5,4,1,128]{4,3,2,1,0:T(1,128)}, s32[3,5,1,128]{3,2,1,0:T(1,128)}) custom-call(f32[13,8,2,1,128]{4,3,2,1,0:T(1,128)} %bitcast.16, f32[8,2,1,128]{3,2,1,0:T(1,128)} %bitcast.17, s32[4,1,128]{2,1,0:T(1,128)} %bitcast.18, f32[4,1,128]{2,1,0:T(1,128)} %bitcast.19, ...), custom_call_target="tpu_custom_call" | custom-call | tf_op jit(solution)/shard_map/pallas_call | solution.py:404
  27.4 12.7 %shard_map.56 = f32[125,1,256]{2,1,0:T(1,128)} custom-call(s32[3,5,1,128]{3,2,1,0:T(1,128)} %get-tuple-element.9.n_any, f32[14,7,16,128]{3,2,1,0:T(8,128)} %bitcast.15, s32[3,5,4,1,128]{4,3,2,1,0:T(1,128)} %get-tuple-element.11.fc_any, f32[3,5,4,1,128]{4,3,2,1,0:T(1,128)} %get-tuple-element.12.ft_any), custom_call_target="tpu_custom_call" | custom-call | tf_op jit(solution)/shard_map/pallas_call | solution.py:431

commit v4 on v3

--- a/solution.py
+++ b/solution.py
@@ -29,7 +29,7 @@
     return (dx + 1) * 9 + (dy + 1) * 3 + dz + 1
 
 
-def body(n_any, c_any, fc_any, ft_any, out_ref, counts, c_ref, fc_ref, ft_ref, sems, kf, inv_ref, fd, pat, bands, fp, gs, s3, ap, b3, acc_ref, cols):
+def body(n_any, c_any, fc_any, ft_any, out_ref, counts, c_ref, fc_ref, ft_ref, sems, kf, inv_ref, fd, pat, bands, fp, gs, s3, b3, acc_ref, cols):
     loads = []
     for n, (a, b) in enumerate(
         ((n_any, counts), (fc_any, fc_ref), (ft_any, ft_ref), (c_any, c_ref))
@@ -160,19 +160,19 @@
                 tile = tile + gs[x, r, 1, pl.ds(y + 1, 1), :] * pat[8]
                 tile = tile + gs[x, r, 2, pl.ds(y + 1, 1), :] * pat[9]
                 s3[1, x, y, r] = tile
+                s3[0, x, y, r] = pltpu.roll(tile, 1, 1)
+                s3[2, x, y, r] = pltpu.roll(tile, 127, 1)
         ry = 1 - lax.rem(y, 2)
         for side, xs in enumerate((x_own, x_par, x_oth)):
             rx = xs & 1
             iv = inv_ref[xs + 2, pl.ds(y + 1, 1), :] * F32(damping * tent)
-            s3[1, xs + 2, y, rx * 2 + ry] += iv * fp[side, y]
-        for x in range(6):
-            for r in range(4):
-                tile = s3[1, x, y, r]
-                s3[0, x, y, r] = pltpu.roll(tile, 1, 1)
-                s3[2, x, y, r] = pltpu.roll(tile, 127, 1)
+            tile = s3[1, xs + 2, y, rx * 2 + ry] + iv * fp[side, y]
+            s3[1, xs + 2, y, rx * 2 + ry] = tile
+            s3[0, xs + 2, y, rx * 2 + ry] = pltpu.roll(tile, 1, 1)
+            s3[2, xs + 2, y, rx * 2 + ry] = pltpu.roll(tile, 127, 1)
         return carry
 
-    lax.fori_loop(0, 12, smooth, 0)
+    lax.fori_loop(0, 12, smooth, 0, unroll=2)
 
     def apply_pair(t, carry):
         for x in range(-1, 3):
@@ -191,46 +191,43 @@
                                     q = (bx + rx) * 3 + by + ry
                                     v = row * s3[dz + 1, xn + 2, 2 * t + yn + 2, rx * 2 + ry]
                                     acc[q] = v if acc[q] is None else acc[q] + v
+                iv = inv_ref[x + 2, pl.ds(2 * t + y + 3, 1), :]
                 for q in range(9):
-                    ap[x + 1, 2 * t + y + 1, q] = acc[q]
+                    tile = acc[q] * iv
+                    b3[x + 1, 2 * t + y + 1, q] = tile
         return carry
 
     lax.fori_loop(0, 5, apply_pair, 0)
 
     def apply_fault(n, carry):
-        y = n - 1
-        y_is_odd = y & 1
+        y_is_odd = (n - 1) & 1
         for side, (xs, xn) in enumerate(((x_own, x_par), (x_par, x_own))):
-            for rx in range(2):
-                for ry in range(2):
-                    tile = s3[1, xn + 2, n + 1, rx * 2 + ry]
-                    total = jnp.zeros((8, 128), F32)
-                    for d in range(17):
-                        row = bands[side, n + 1, d : d + 1, :]
-                        total = total + row * pltpu.roll(tile, (8 - d) % 128, 1)
-                    q = ((xs & 1) + rx) * 3 + y_is_odd + ry
-                    ap[xs + 1, n, q] -= total
-        for x in range(4):
-            iv = inv_ref[x + 1, pl.ds(n + 2, 1), :]
-            for q in range(9):
-                tile = ap[x, n, q] * iv
-                b3[1, x, n, q] = tile
-                b3[0, x, n, q] = pltpu.roll(tile, 1, 1)
-                b3[2, x, n, q] = pltpu.roll(tile, 127, 1)
+            iv = inv_ref[xs + 2, pl.ds(n + 2, 1), :]
+            done = []
+            for r in range(4):
+                tile = s3[1, xn + 2, n + 1, r]
+                total = jnp.zeros((8, 128), F32)
+                for d in range(17):
+                    row = bands[side, n + 1, d : d + 1, :]
+                    total = total + row * pltpu.roll(tile, (8 - d) % 128, 1)
+                q = ((xs & 1) + r // 2) * 3 + y_is_odd + r % 2
+                done.append((q, b3[xs + 1, n, q] - total * iv))
+            for q, tile in done:
+                b3[xs + 1, n, q] = tile
         return carry
 
-    lax.fori_loop(0, 10, apply_fault, 0)
+    lax.fori_loop(0, 10, apply_fault, 0, unroll=2)
 
     pz = lax.broadcasted_iota(jnp.int32, (128, 64), 0)
     pc = lax.broadcasted_iota(jnp.int32, (128, 64), 1)
     pick = jnp.where(lax.shift_right_logical(pz, 1) == pc, F32(tent), F32(0.0))
 
     def restrict(yc, carry):
-        acc = [None] * 25
-        for xn in range(-1, 3):
-            for yn in range(-1, 3):
-                bx, by = xn // 2 + 1, yn // 2 + 1
-                for dz in (-1, 0, 1):
+        for dz in (-1, 1, 0):
+            acc = [None] * 25
+            for xn in range(-1, 3):
+                for yn in range(-1, 3):
+                    bx, by = xn // 2 + 1, yn // 2 + 1
                     row = None
                     for x in (0, 1):
                         for y in (0, 1):
@@ -240,38 +237,43 @@
                     row = row * F32(-damping)
                     if dz == 0 and xn in (0, 1) and yn in (0, 1):
                         row = row + kf[13, xn + 2, pl.ds(2 * yc + yn + 3, 1), :]
+                    row = jnp.broadcast_to(row, (8, 128))
+                    if dz:
+                        row = pltpu.roll(row, dz % 128, 1)
                     for rx in range(3):
                         for ry in range(3):
                             q = (bx + rx) * 5 + by + ry
-                            v = row * b3[dz + 1, xn + 1, 2 * yc + yn + 1, rx * 3 + ry]
+                            v = row * b3[xn + 1, 2 * yc + yn + 1, rx * 3 + ry]
                             acc[q] = v if acc[q] is None else acc[q] + v
-        for q in range(25):
-            acc_ref[q // 5, q % 5] = acc[q]
+            for q in range(25):
+                v = pltpu.roll(acc[q], -dz % 128, 1) if dz else acc[q]
+                acc_ref[yc, q // 5, q % 5] = v if dz == -1 else acc_ref[yc, q // 5, q % 5] + v
         far = lax.shift_right_arithmetic(x_par, 1) + 1
         for rx in range(3):
             for ry in range(3):
                 total = jnp.zeros((8, 128), F32)
                 for y in range(2):
-                    tile = b3[1, x_par + 1, 2 * yc + y + 1, rx * 3 + ry]
+                    tile = b3[x_par + 1, 2 * yc + y + 1, rx * 3 + ry]
                     for d in range(17):
                         row = bands[0, 2 * yc + y + 2, d : d + 1, :]
                         total = total + row * pltpu.roll(tile, (8 - d) % 128, 1)
-                acc_ref[far + rx, 1 + ry] += total * F32(damping)
-        got = jnp.dot(
-            acc_ref[...].reshape(200, 128),
-            pick,
-            precision=lax.Precision.HIGHEST,
-            preferred_element_type=F32,
-        )
+                acc_ref[yc, far + rx, 1 + ry] += total * F32(damping)
+        return carry
+
+    lax.fori_loop(0, 4, restrict, 0)
+    got = jnp.dot(
+        acc_ref[...].reshape(800, 128),
+        pick,
+        precision=lax.Precision.HIGHEST,
+        preferred_element_type=F32,
+    )
+    for yc in range(4):
         for rx in range(5):
             a = lax.rem(gx + rx + 3, 5)
             for ry in range(5):
                 b = lax.rem(gy * 4 + yc + ry + 3, 5)
-                q = (rx * 5 + ry) * 8
+                q = (yc * 25 + rx * 5 + ry) * 8
                 cols[a, b, yc] = got[q : q + 8]
-        return carry
-
-    lax.fori_loop(0, 4, restrict, 0)
     for a in range(5):
         for b in range(5):
             tile = jnp.concatenate([cols[a, b, yc] for yc in range(4)], axis=1)
@@ -448,8 +450,7 @@
             pltpu.VMEM((6, 4, 3, 16, 128), F32),
             pltpu.VMEM((3, 6, 12, 4, 8, 128), F32),
             pltpu.VMEM((4, 10, 9, 8, 128), F32),
-            pltpu.VMEM((3, 4, 10, 9, 8, 128), F32),
-            pltpu.VMEM((5, 5, 8, 128), F32),
+            pltpu.VMEM((4, 5, 5, 8, 128), F32),
             pltpu.VMEM((5, 5, 4, 8, 64), F32),
         ],
         compiler_params=pltpu.CompilerParams(vmem_limit_bytes=67043328),

time: 40.3 us -> 40.5 us (level)
  no operation moved by 1% of the time
where the time goes in v4:
time: 40.5 us; the launch traced here: 40.4 us
  Pallas kernels  39.1 us (97%)
  between operations  0.66 us (2%)
  local copies, waits for them, and re-layouts  0.58 us (1%)
    pallas_call x1, Pallas kernels, per_device(): pl.pallas_call(exchange, out_shape=(jax.ShapeDtypeStruct((14, 7, 16, 1, 1...  26.1 us
    pallas_call x1, Pallas kernels, per_device(): pl.pallas_call(body, out_shape=jax.ShapeDtypeStruct((125, 1, 256), F32),...  13 us

profile of v4, /device:TPU:17, one launch (start us, length us, event | category | flops | bytes accessed | tf_op | source)
XLA Modules:
  0.0 40.4 jit_solution(18427931735459208417)
XLA Ops:
  0.7 0.6 %broadcast_in_dim.8.count = s32[1,128]{1,0:T(1,128)} broadcast(s32[]{:T(128)} %bitcast.14), dimensions={} | broadcast | bytes 516 | tf_op jit(solution)/shard_map/broadcast_in_dim | solution.py:431
  1.2 26.1 %shard_map.55 = (f32[14,7,16,1,128]{4,3,2,1,0:T(1,128)}, s32[3,5,4,1,128]{4,3,2,1,0:T(1,128)}, f32[3,5,4,1,128]{4,3,2,1,0:T(1,128)}, s32[3,5,1,128]{3,2,1,0:T(1,128)}) custom-call(f32[13,8,2,1,128]{4,3,2,1,0:T(1,128)} %bitcast.16, f32[8,2,1,128]{3,2,1,0:T(1,128)} %bitcast.17, s32[4,1,128]{2,1,0:T(1,128)} %bitcast.18, f32[4,1,128]{2,1,0:T(1,128)} %bitcast.19, ...), custom_call_target="tpu_custom_call" | custom-call | tf_op jit(solution)/shard_map/pallas_call | solution.py:406
  27.4 13.0 %shard_map.56 = f32[125,1,256]{2,1,0:T(1,128)} custom-call(s32[3,5,1,128]{3,2,1,0:T(1,128)} %get-tuple-element.9.n_any, f32[14,7,16,128]{3,2,1,0:T(8,128)} %bitcast.15, s32[3,5,4,1,128]{4,3,2,1,0:T(1,128)} %get-tuple-element.11.fc_any, f32[3,5,4,1,128]{4,3,2,1,0:T(1,128)} %get-tuple-element.12.ft_any), custom_call_target="tpu_custom_call" | custom-call | tf_op jit(solution)/shard_map/pallas_call | solution.py:433

commit v5 on v4

--- a/solution.py
+++ b/solution.py
@@ -120,13 +120,17 @@
             bands[side, yout : yout + ny] = got.reshape(ny, 24, 128)
 
     fd[...] = jnp.zeros((6, 16, 128), F32)
-    for side, xs in enumerate((x_own, x_par, x_oth)):
-        for y in range(12):
+
+    def probe_fault(y, carry):
+        for side, xs in enumerate((x_own, x_par, x_oth)):
             tile = jnp.zeros((8, 128), F32)
             for d in range(17):
                 tile = tile + bands[side, y, d : d + 1, :] * pat[d]
             fp[side, y] = tile
-            fd[xs + 2, y + 1 : y + 2, :] = jnp.sum(tile, axis=0, keepdims=True)
+            fd[xs + 2, pl.ds(y + 1, 1), :] = jnp.sum(tile, axis=0, keepdims=True)
+        return carry
+
+    lax.fori_loop(0, 12, probe_fault, 0)
 
     for x in range(-2, 4):
         diag = c_ref[13, x + 3] + wsum[x + 2] + fd[x + 2]
@@ -172,7 +176,7 @@
             s3[2, xs + 2, y, rx * 2 + ry] = pltpu.roll(tile, 127, 1)
         return carry
 
-    lax.fori_loop(0, 12, smooth, 0, unroll=2)
+    lax.fori_loop(0, 12, smooth, 0)
 
     def apply_pair(t, carry):
         for x in range(-1, 3):
@@ -216,7 +220,7 @@
                 b3[xs + 1, n, q] = tile
         return carry
 
-    lax.fori_loop(0, 10, apply_fault, 0, unroll=2)
+    lax.fori_loop(0, 10, apply_fault, 0)
 
     pz = lax.broadcasted_iota(jnp.int32, (128, 64), 0)
     pc = lax.broadcasted_iota(jnp.int32, (128, 64), 1)

time: 40.5 us -> 41.8 us (1.032)
  Pallas kernels: 39.1 us -> 40.4 us
    pallas_call x1, Pallas kernels: 13 us -> 14.2 us  [per_device(): pl.pallas_call(body, out_shape=jax.ShapeDtypeStruct((125, 1, 256), F32),...]
where the time goes in v5:
time: 41.8 us; the launch traced here: 41.6 us
  Pallas kernels  40.4 us (97%)
  between operations  0.66 us (2%)
  local copies, waits for them, and re-layouts  0.58 us (1%)
    pallas_call x1, Pallas kernels, per_device(): pl.pallas_call(exchange, out_shape=(jax.ShapeDtypeStruct((14, 7, 16, 1, 1...  26.1 us
    pallas_call x1, Pallas kernels, per_device(): pl.pallas_call(body, out_shape=jax.ShapeDtypeStruct((125, 1, 256), F32),...  14.2 us

profile of v5, /device:TPU:17, one launch (start us, length us, event | category | flops | bytes accessed | tf_op | source)
XLA Modules:
  0.0 41.6 jit_solution(11580947354944952730)
XLA Ops:
  0.7 0.6 %broadcast_in_dim.8.count = s32[1,128]{1,0:T(1,128)} broadcast(s32[]{:T(128)} %bitcast.14), dimensions={} | broadcast | bytes 516 | tf_op jit(solution)/shard_map/broadcast_in_dim | solution.py:435
  1.2 26.1 %shard_map.55 = (f32[14,7,16,1,128]{4,3,2,1,0:T(1,128)}, s32[3,5,4,1,128]{4,3,2,1,0:T(1,128)}, f32[3,5,4,1,128]{4,3,2,1,0:T(1,128)}, s32[3,5,1,128]{3,2,1,0:T(1,128)}) custom-call(f32[13,8,2,1,128]{4,3,2,1,0:T(1,128)} %bitcast.16, f32[8,2,1,128]{3,2,1,0:T(1,128)} %bitcast.17, s32[4,1,128]{2,1,0:T(1,128)} %bitcast.18, f32[4,1,128]{2,1,0:T(1,128)} %bitcast.19, ...), custom_call_target="tpu_custom_call" | custom-call | tf_op jit(solution)/shard_map/pallas_call | solution.py:410
  27.4 14.2 %shard_map.56 = f32[125,1,256]{2,1,0:T(1,128)} custom-call(s32[3,5,1,128]{3,2,1,0:T(1,128)} %get-tuple-element.9.n_any, f32[14,7,16,128]{3,2,1,0:T(8,128)} %bitcast.15, s32[3,5,4,1,128]{4,3,2,1,0:T(1,128)} %get-tuple-element.11.fc_any, f32[3,5,4,1,128]{4,3,2,1,0:T(1,128)} %get-tuple-element.12.ft_any), custom_call_target="tpu_custom_call" | custom-call | tf_op jit(solution)/shard_map/pallas_call | solution.py:437
